TPU v7x, 256 devices: a whole 4x4x8 slice. The times are simulated.
256 devices in a mesh: section: 16 (over x_hi, z), lane: 16 (over y, x_lo, core).
Axes of the slice: x: 4 (x_hi: 2, x_lo: 2; x = x_hi * 2 + x_lo), y: 4, z: 8, core: 2. Of those that a mesh axis runs over, the one named last changes fastest.
Arguments:
- value_weight: float32 [16, 1024, 256], P('section', 'lane'), may hold values from -0.1875 to 0.1875
- out_weight: float32 [16, 2048, 1024], P('section', 'lane'), may hold values from -0.125 to 0.125
- value_moment: float32 [16, 1024, 256], P('section', 'lane'), may hold values from -6 to 6
- out_moment: float32 [16, 2048, 1024], P('section', 'lane'), may hold values from -6 to 6
- inputs_saved: bfloat16 [2, 2, 16, 2048, 1024], P(None, None, 'section', 'lane'), may hold values from -6 to 6
- queries_saved: bfloat16 [2, 2, 16, 2048, 2048], P(None, None, 'section', 'lane'), may hold values from -100 to 100
- keys_saved: bfloat16 [2, 2, 16, 2048, 256], P(None, None, 'section', 'lane'), may hold values from -5 to 5
- grad_now: bfloat16 [2, 16, 2048, 1024], P(None, 'section', 'lane'), may hold values from -6 to 6
- grad_new: bfloat16 [2, 2048, 1024], P(None, 'lane'), may hold values from -6 to 6
- bound_now: int32 [2, 16, 16], P(None, None, 'lane'), may hold values from 1 to 127
- bound_new: int32 [2, 16], P(None, 'lane'), may hold values from 1 to 127
Outputs:
- grad_inputs: bfloat16 [2, 2, 16, 2048, 1024], P(None, None, 'section', 'lane')
- grad_queries: bfloat16 [2, 2, 16, 2048, 2048], P(None, None, 'section', 'lane')
- grad_keys: bfloat16 [2, 2, 16, 2048, 256], P(None, None, 'section', 'lane')
- value_weight_new: float32 [16, 1024, 256], P('section', 'lane')
- out_weight_new: float32 [16, 2048, 1024], P('section', 'lane')
- value_moment_new: float32 [16, 1024, 256], P('section', 'lane')
- out_moment_new: float32 [16, 2048, 1024], P('section', 'lane')
All inputs are finite; a program needn't handle non-finite values.
Results may differ from a plain program's by a relative error of at most 0.018.
Values may be sent and summed in bfloat16 or wider, within the bound.
A program may use at most 128 MiB of HBM per device.

v0:
```python
import math

import jax
import jax.numpy as jnp
from jax import lax
from jax.sharding import PartitionSpec as P

QUERY_HEAD_COUNT = 16
KEY_VALUE_HEADS = 2
HEAD_SIZE = 128
QW = 2048
KVW = 256


decay_rate = 0.9
learn_rate = 0.01


def side_by_side(arrays, axis, split_dim, concat_dim, along):
    widths = [math.prod(a.shape[along:]) for a in arrays]
    both = jnp.concatenate(
        [a.reshape(*a.shape[:along], w) for a, w in zip(arrays, widths)], axis=along
    )
    whole = lax.all_to_all(both, axis, split_axis=split_dim, concat_axis=concat_dim, tiled=True)
    tiles = jnp.split(whole, [sum(widths[:k]) for k in range(1, len(widths))], axis=along)
    return tuple((b.reshape(*whole.shape[:along], *a.shape[along:]) for a, b in zip(arrays, tiles)))


def for_sending(x):
    return jax.tree.map(lambda a: a.astype(jnp.bfloat16) if a.dtype == jnp.float32 else a, x)


def in_order(tiles, dim):
    lengths = list(tiles.shape[1:])
    lengths[dim] *= tiles.shape[0]
    return jnp.moveaxis(tiles, 0, dim).reshape(lengths)


def one_gather(arrays, axis, dims):
    ravelled = jnp.concatenate([a.reshape(-1) for a in arrays])
    lines, at, gathered = (lax.all_gather(ravelled, axis), 0, [])
    for a, dim in zip(arrays, dims):
        tiles = lines[:, at : at + a.size].reshape(-1, *a.shape)
        gathered.append(in_order(tiles, dim))
        at += a.size
    return tuple(gathered)


def shifted(x, axis, by):
    size = lax.axis_size(axis)
    pairs = [(i, i + by) for i in range(size) if 0 <= i + by < size]
    return lax.ppermute(x, axis, pairs)


def split_up(x, dim, size):
    lengths = x.shape
    tiles = x.reshape(*lengths[:dim], size, lengths[dim] // size, *lengths[dim + 1 :])
    return jnp.moveaxis(tiles, dim, 0)


def sum_together(arrays, axis, dims):
    size = lax.axis_size(axis)
    tiles = [split_up(a, dim, size) for a, dim in zip(arrays, dims)]
    lines = jnp.concatenate([b.reshape(size, -1) for b in tiles], axis=1)
    width = max(16, -(-lines.shape[1] // 1024) * 8)
    lines = jnp.pad(lines, ((0, 0), (0, width * 128 - lines.shape[1]))).reshape(-1, 128)
    ravelled, at, gathered = (lax.psum_scatter(lines, axis, tiled=True).reshape(-1), 0, [])
    for b in tiles:
        part = b[0]
        gathered.append(ravelled[at : at + part.size].reshape(part.shape))
        at += part.size
    return tuple(gathered)


def backward(inputs, query_rows, key_rows, cotangent, bound, w_value, w_out):
    token_rows = inputs.shape[0]
    query_group = QUERY_HEAD_COUNT // KEY_VALUE_HEADS
    scale_factor = 1.0 / math.sqrt(HEAD_SIZE)
    value_matrix = jnp.dot(inputs, w_value, preferred_element_type=jnp.float32).astype(jnp.bfloat16)
    heads_of_query = query_rows.reshape(token_rows, KEY_VALUE_HEADS, query_group, HEAD_SIZE)
    heads_of_key = key_rows.reshape(token_rows, KEY_VALUE_HEADS, HEAD_SIZE)
    heads_of_value = value_matrix.reshape(token_rows, KEY_VALUE_HEADS, HEAD_SIZE)
    scores = (
        jnp.einsum(
            "ihgd,jhd->hgij", heads_of_query, heads_of_key, preferred_element_type=jnp.float32
        )
        * scale_factor
    )
    places = jnp.arange(token_rows)
    second = places >= bound
    allowed = (places[None, :] <= places[:, None]) & (second[:, None] == second[None, :])
    scores = jnp.where(allowed[None, None], scores, -1e30)
    top_score = jnp.max(scores, axis=-1, keepdims=True)
    expo = jnp.exp(scores - top_score)
    probs = expo / jnp.sum(expo, axis=-1, keepdims=True)
    probs_low = probs.astype(jnp.bfloat16)
    attended = (
        jnp.einsum("hgij,jhd->ihgd", probs_low, heads_of_value, preferred_element_type=jnp.float32)
        .astype(jnp.bfloat16)
        .reshape(token_rows, QW)
    )
    attended_gradient = jnp.einsum(
        "td,cd->tc", cotangent, w_out, preferred_element_type=jnp.float32
    ).astype(jnp.bfloat16)
    head_gradient = attended_gradient.reshape(token_rows, KEY_VALUE_HEADS, query_group, HEAD_SIZE)
    grad_values = (
        jnp.einsum("hgij,ihgd->jhd", probs_low, head_gradient, preferred_element_type=jnp.float32)
        .astype(jnp.bfloat16)
        .reshape(token_rows, KVW)
    )
    grad_inputs = (
        cotangent.astype(jnp.float32)
        + jnp.einsum("tc,dc->td", grad_values, w_value, preferred_element_type=jnp.float32)
    ).astype(jnp.bfloat16)
    grad_probs = jnp.einsum(
        "ihgd,jhd->hgij", head_gradient, heads_of_value, preferred_element_type=jnp.float32
    )
    delta = jnp.sum(probs * grad_probs, axis=-1, keepdims=True)
    grad_scores = (probs * (grad_probs - delta) * scale_factor).astype(jnp.bfloat16)
    grad_queries = (
        jnp.einsum("hgij,jhd->ihgd", grad_scores, heads_of_key, preferred_element_type=jnp.float32)
        .astype(jnp.bfloat16)
        .reshape(token_rows, QW)
    )
    grad_keys = (
        jnp.einsum(
            "hgij,ihgd->jhd", grad_scores, heads_of_query, preferred_element_type=jnp.float32
        )
        .astype(jnp.bfloat16)
        .reshape(token_rows, KVW)
    )
    grad_wvalue = jnp.einsum("td,tc->dc", inputs, grad_values, preferred_element_type=jnp.float32)
    grad_wout = jnp.einsum("tc,td->cd", attended, cotangent, preferred_element_type=jnp.float32)
    return (grad_inputs, grad_queries, grad_keys, grad_wvalue, grad_wout)


def fold_columns(array, sections):
    count, width = array.shape
    return array.reshape(count, sections, width // sections).transpose(1, 0, 2)


def unfold_columns(array):
    sections, count, width = array.shape
    return array.transpose(1, 0, 2).reshape(count, sections * width)


def mirror_weights(value_rows, out_rows):
    sections = lax.axis_size("section")
    spread_value, spread_out = side_by_side(
        (fold_columns(value_rows, sections), fold_columns(out_rows, sections)), "section", 0, 0, 1
    )
    got_value, got_out = side_by_side((spread_value[::-1], spread_out[::-1]), "section", 0, 0, 1)
    return (unfold_columns(got_value), unfold_columns(got_out))


def mirror_gradients(value_rows, out_rows):
    sections = lax.axis_size("section")
    spread_value, spread_out = tuple(
        (
            part.astype(jnp.float32)
            for part in side_by_side(
                (
                    fold_columns(value_rows, sections).astype(jnp.bfloat16),
                    fold_columns(out_rows, sections).astype(jnp.bfloat16),
                ),
                "section",
                0,
                0,
                1,
            )
        )
    )
    got_value, got_out = (
        lax.all_to_all(
            for_sending(spread_value[::-1]), "section", split_axis=0, concat_axis=0, tiled=True
        ),
        lax.all_to_all(
            for_sending(spread_out[::-1]), "section", split_axis=0, concat_axis=0, tiled=True
        ),
    )
    return (unfold_columns(got_value), unfold_columns(got_out))


def shards(
    value_weight,
    out_weight,
    value_moment,
    out_moment,
    inputs_saved,
    queries_saved,
    keys_saved,
    grad_now,
    grad_new,
    bound_now,
    bound_new,
):
    sections = lax.axis_size("section")
    relay_lanes = lax.axis_size("lane")
    place = lax.axis_index("section")
    own_value = value_weight[0].astype(jnp.bfloat16)
    own_out = out_weight[0].astype(jnp.bfloat16)
    value_first, output_first = (
        lax.all_gather(own_value, "lane", axis=0, tiled=True),
        lax.all_gather(own_out, "lane", axis=0, tiled=True),
    )
    mirror_value, mirror_out = mirror_weights(own_value, own_out)
    value_second, output_second = one_gather((mirror_value, mirror_out), "lane", (0, 0))
    early_first = backward(
        inputs_saved[0, 0, 0],
        queries_saved[0, 0, 0],
        keys_saved[0, 0, 0],
        grad_now[0, 0],
        bound_now[0, place, 0],
        value_first,
        output_first,
    )
    early_second = backward(
        inputs_saved[1, 0, 0],
        queries_saved[1, 0, 0],
        keys_saved[1, 0, 0],
        grad_now[1, 0],
        bound_now[1, place, 0],
        value_second,
        output_second,
    )
    arrived_first = shifted(early_first[0], "section", -1)
    arrived_second = shifted(early_second[0], "section", 1)
    at_tail = place == sections - 1
    cot_first = jnp.where(at_tail, grad_new[0], arrived_first)
    bound_first = jnp.where(
        at_tail, bound_new[0, 0], bound_now[0, jnp.minimum(place + 1, sections - 1), 0]
    )
    at_head = place == 0
    cot_second = jnp.where(at_head, grad_new[1], arrived_second)
    bound_second = jnp.where(at_head, bound_new[1, 0], bound_now[1, jnp.maximum(place - 1, 0), 0])
    late_first = backward(
        inputs_saved[0, 1, 0],
        queries_saved[0, 1, 0],
        keys_saved[0, 1, 0],
        cot_first,
        bound_first,
        value_first,
        output_first,
    )
    late_second = backward(
        inputs_saved[1, 1, 0],
        queries_saved[1, 1, 0],
        keys_saved[1, 1, 0],
        cot_second,
        bound_second,
        value_second,
        output_second,
    )
    term_value_first = early_first[3] + late_first[3]
    term_out_first = early_first[4] + late_first[4]
    term_value_second = early_second[3] + late_second[3]
    term_out_second = early_second[4] + late_second[4]
    sum_value_first, sum_out_first = tuple(
        (
            part.astype(jnp.float32)
            for part in sum_together(
                (term_value_first.astype(jnp.bfloat16), term_out_first.astype(jnp.bfloat16)),
                "lane",
                (0, 0),
            )
        )
    )
    sum_value_second, sum_out_second = tuple(
        (
            part.astype(jnp.float32)
            for part in sum_together(
                (term_value_second.astype(jnp.bfloat16), term_out_second.astype(jnp.bfloat16)),
                "lane",
                (0, 0),
            )
        )
    )
    back_value, back_out = mirror_gradients(sum_value_second, sum_out_second)
    mean_value = (sum_value_first + back_value) / relay_lanes
    mean_out = (sum_out_first + back_out) / relay_lanes
    value_moment_new = decay_rate * value_moment + mean_value[None]
    out_moment_new = decay_rate * out_moment + mean_out[None]
    value_weight_new = value_weight - learn_rate * value_moment_new
    out_weight_new = out_weight - learn_rate * out_moment_new
    grad_inputs = jnp.stack(
        [jnp.stack([early_first[0], late_first[0]]), jnp.stack([early_second[0], late_second[0]])]
    )[:, :, None]
    grad_queries = jnp.stack(
        [jnp.stack([early_first[1], late_first[1]]), jnp.stack([early_second[1], late_second[1]])]
    )[:, :, None]
    grad_keys = jnp.stack(
        [jnp.stack([early_first[2], late_first[2]]), jnp.stack([early_second[2], late_second[2]])]
    )[:, :, None]
    return (
        grad_inputs,
        grad_queries,
        grad_keys,
        value_weight_new,
        out_weight_new,
        value_moment_new,
        out_moment_new,
    )


def solution(mesh):
    return jax.shard_map(
        shards,
        mesh=mesh,
        in_specs=(
            P("section", "lane", None),
            P("section", "lane", None),
            P("section", "lane", None),
            P("section", "lane", None),
            P(None, None, "section", "lane", None),
            P(None, None, "section", "lane", None),
            P(None, None, "section", "lane", None),
            P(None, "section", "lane", None),
            P(None, "lane", None),
            P(None, None, "lane"),
            P(None, "lane"),
        ),
        out_specs=(
            P(None, None, "section", "lane", None),
            P(None, None, "section", "lane", None),
            P(None, None, "section", "lane", None),
            P("section", "lane", None),
            P("section", "lane", None),
            P("section", "lane", None),
            P("section", "lane", None),
        ),
        check_vma=False,
    )
```

profile of v0, /device:TPU:32, one launch (start us, length us, event | category | flops | bytes accessed | tf_op | source)
XLA Modules:
  0.0 381.5 jit_solution(7223138236569754382)
XLA Ops:
  13.8 22.9 %all_to_all.46 = bf16[16,2,4608]{2,1,0:T(2,128)(2,1)S(1)} all-to-all(bf16[16,2,4608]{2,1,0:T(2,128)(2,1)S(1)} %reshape.458), channel_id=1, replica_groups=mesh['section'=16,'lane'=16] {'section'}, dimensions={0} | all-to-all | bytes 589824 | tf_op jit(solution)/shard_map/all_to_all | solution.py:24
  39.7 16.3 %all_to_all.47 = bf16[16,2,4608]{2,1,0:T(2,128)(2,1)S(1)} all-to-all(bf16[16,2,4608]{2,1,0:T(2,128)(2,1)S(1)} %reshape.460), channel_id=1, replica_groups=mesh['section'=16,'lane'=16] {'section'}, dimensions={0} | all-to-all | bytes 589824 | tf_op jit(solution)/shard_map/all_to_all | solution.py:24
  59.5 21.6 %all-gather.1 = bf16[1,1024,256]{2,1,0:T(8,128)(2,1)S(1)} all-gather(bf16[1,64,256]{2,1,0:T(8,128)(2,1)S(1)} %convert_element_type.318), channel_id=3, replica_groups=mesh['section'=16,'lane'=16] {'lane'}, dimensions={1}, use_global_device_ids=true | all-gather | bytes 557056 | tf_op jit(solution)/shard_map/all_gather | solution.py:203
  108.0 4.5 %fusion.118 = f32[2048,1024]{1,0:T(8,128)} fusion(bf16[128,2048]{0,1:T(8,128)(2,1)S(1)} %bitcast.408, bf16[2,1,128,1024]{3,2,1,0:T(8,128)(2,1)S(1)} %copy-done.3), kind=kOutput, calls=%fused_computation.171 | convolution fusion | flops 536870912 | bytes 9175040 | tf_op jit(solution)/shard_map/tc,td->cd/dot_general | solution.py:133
  120.5 5.0 %reshape.433 = bf16[16,147456]{1,0:T(8,128)(2,1)} reshape(bf16[2359296]{0:T(1024)(128)(2,1)} %all-gather.8.cloned.1.call-done) | data formatting | bytes 9437184 | tf_op jit(solution)/shard_map/all_gather | solution.py:41
  125.6 4.5 %slice.100 = bf16[16,131072]{1,0:T(8,128)(2,1)} slice(bf16[16,147456]{1,0:T(8,128)(2,1)} %reshape.433), slice={[0:16], [16384:147456]} | slice | bytes 8388608 | tf_op jit(solution)/shard_map/slice | solution.py:43
  134.2 5.0 %reshape_reshape.26 = bf16[2048,1024]{1,0:T(8,128)(2,1)} reshape(bf16[16,131072]{1,0:T(8,128)(2,1)} %slice.100) | data formatting | bytes 8388608 | tf_op jit(solution)/shard_map/reshape;reshape | solution.py:36
  139.1 4.2 %convolution_convert_fusion.1 = bf16[2048,128]{1,0:T(8,128)(2,1)} fusion(bf16[2048,1024]{1,0:T(8,128)(2,1)} %reshape_reshape.26, bf16[2,1,128,1024]{3,2,1,0:T(8,128)(2,1)S(1)} %copy-done.4), kind=kOutput, calls=%fused_computation.19 | convolution fusion | flops 537133056 | bytes 4980736 | tf_op jit(solution)/shard_map/td,cd->tc/dot_general | solution.py:102
  149.8 3.7 collective-permute-start.1
  153.6 5.7 %fusion.115 = f32[2048,1024]{1,0:T(8,128)} fusion(bf16[128,2048]{0,1:T(8,128)(2,1)} %bitcast.421, bf16[2,1,128,1024]{3,2,1,0:T(8,128)(2,1)S(1)} %copy-done.4), kind=kOutput, calls=%fused_computation.167 | convolution fusion | flops 536870912 | bytes 9175040 | tf_op jit(solution)/shard_map/tc,td->cd/dot_general | solution.py:133
  179.4 6.6 %add_convert_fusion = bf16[2048,1024]{1,0:T(8,128)(2,1)} fusion(f32[2048,1024]{1,0:T(8,128)} %fusion.115, bf16[128,2048]{0,1:T(8,128)(2,1)S(1)} %bitcast.417, bf16[128,1024]{1,0:T(8,128)(2,1)S(1)} %get-tuple-element.58), kind=kOutput, calls=%fused_computation.8 | convolution fusion | flops 541065216 | bytes 13369344 | tf_op jit(solution)/shard_map/tc,td->cd/dot_general | solution.py:133
  186.0 4.9 %reshape_reshape.31 = bf16[16,131072]{1,0:T(8,128)(2,1)} reshape(bf16[2048,1024]{1,0:T(8,128)(2,1)} %add_convert_fusion) | data formatting | bytes 8388608 | tf_op jit(solution)/shard_map/reshape;reshape | solution.py:64
  190.9 4.2 %pad_maximum_fusion.1 = bf16[16,147456]{1,0:T(8,128)(2,1)} fusion(bf16[16,131072]{1,0:T(8,128)(2,1)} %reshape_reshape.31, bf16[16,16384]{1,0:T(8,128)(2,1)S(1)} %copy-done.13), kind=kLoop, calls=%fused_computation.11 | loop fusion | flops 9437184 | bytes 9437184 | tf_op jit(solution)/shard_map/concatenate | solution.py:64
  195.1 5.3 %reshape.422 = bf16[18432,128]{1,0:T(8,128)(2,1)} reshape(bf16[16,147456]{1,0:T(8,128)(2,1)} %pad_maximum_fusion.1) | data formatting | bytes 9437184 | tf_op jit(solution)/shard_map/reshape | solution.py:66
  201.4 6.5 %add_convert_fusion.1 = bf16[2048,1024]{1,0:T(8,128)(2,1)} fusion(f32[2048,1024]{1,0:T(8,128)} %fusion.118, bf16[128,2048]{0,1:T(8,128)(2,1)S(1)} %bitcast.412, bf16[128,1024]{1,0:T(8,128)(2,1)S(1)} %get-tuple-element.57), kind=kOutput, calls=%fused_computation.9 | convolution fusion | flops 541065216 | bytes 13369344 | tf_op jit(solution)/shard_map/tc,td->cd/dot_general | solution.py:133
  208.0 5.0 %reshape_reshape.29 = bf16[16,131072]{1,0:T(8,128)(2,1)} reshape(bf16[2048,1024]{1,0:T(8,128)(2,1)} %add_convert_fusion.1) | data formatting | bytes 8388608 | tf_op jit(solution)/shard_map/reshape;reshape | solution.py:64
  213.0 4.3 %pad_maximum_fusion = bf16[16,147456]{1,0:T(8,128)(2,1)} fusion(bf16[16,131072]{1,0:T(8,128)(2,1)} %reshape_reshape.29, bf16[16,16384]{1,0:T(8,128)(2,1)S(1)} %reshape_reshape.28), kind=kLoop, calls=%fused_computation.10 | loop fusion | flops 9437184 | bytes 9437184 | tf_op jit(solution)/shard_map/concatenate | solution.py:64
  217.2 5.3 %reshape.419 = bf16[18432,128]{1,0:T(8,128)(2,1)} reshape(bf16[16,147456]{1,0:T(8,128)(2,1)} %pad_maximum_fusion) | data formatting | bytes 9437184 | tf_op jit(solution)/shard_map/reshape | solution.py:66
  280.4 8.0 %all-to-all-start.2 = ((bf16[16,2,4608]{2,1,0:T(2,128)(2,1)}), bf16[16,2,4608]{2,1,0:T(2,128)(2,1)S(1)}, u32[]{:S(2)}, u32[]{:S(2)}) async-start(bf16[16,2,4608]{2,1,0:T(2,128)(2,1)} %reshape.462), calls=%async_computation.4 | async-start | bytes 589824 | tf_op jit(solution)/shard_map/all_to_all | solution.py:24
  290.1 9.8 %all-to-all-done.2 = bf16[16,2,4608]{2,1,0:T(2,128)(2,1)S(1)} async-done(((bf16[16,2,4608]{2,1,0:T(2,128)(2,1)}), bf16[16,2,4608]{2,1,0:T(2,128)(2,1)S(1)}, u32[]{:S(2)}, u32[]{:S(2)}) %all-to-all-start.2) | async-done | bytes 294944 | tf_op jit(solution)/shard_map/all_to_all | solution.py:24
  301.4 4.8 %all-to-all-start.3 = ((bf16[16,2,512]{2,1,0:T(2,128)(2,1)}), bf16[16,2,512]{2,1,0:T(2,128)(2,1)S(1)}, u32[]{:S(2)}, u32[]{:S(2)}) async-start(bf16[16,2,512]{2,1,0:T(2,128)(2,1)} %reshape.464), calls=%async_computation.5 | async-start | bytes 65536 | tf_op jit(solution)/shard_map/all_to_all | solution.py:174
  306.2 44.4 %reduce-scatter.3.cloned.1.call-done = bf16[1152,128]{1,0:T(8,128)(2,1)} async-done(((bf16[18432,128]{1,0:T(8,128)(2,1)}), bf16[1152,128]{1,0:T(8,128)(2,1)}) %reduce-scatter.3.cloned.1.call-update) | async-done | bytes 294928 | tf_op jit(solution)/shard_map/reduce_scatter | solution.py:67
  353.1 9.6 %all-to-all-start.4 = ((bf16[16,128,64]{1,2,0:T(8,128)(2,1)}), bf16[16,128,64]{1,2,0:T(8,128)(2,1)S(1)}, u32[]{:S(2)}, u32[]{:S(2)}) async-start(bf16[16,128,64]{1,2,0:T(8,128)(2,1)} %rev.18), calls=%async_computation.6 | async-start | bytes 524288 | tf_op jit(solution)/shard_map/all_to_all | solution.py:177
  364.5 8.8 %all-to-all-done.4 = bf16[16,128,64]{1,2,0:T(8,128)(2,1)S(1)} async-done(((bf16[16,128,64]{1,2,0:T(8,128)(2,1)}), bf16[16,128,64]{1,2,0:T(8,128)(2,1)S(1)}, u32[]{:S(2)}, u32[]{:S(2)}) %all-to-all-start.4) | async-done | bytes 262176 | tf_op jit(solution)/shard_map/all_to_all | solution.py:177
  (286 shorter events, 143.2 us)
Async XLA Ops:
  7.2 105.3 %all-gather.6.cloned.1.call-start = ((), (), s32[]{:S(2)}) async-start(), calls=%async_computation.9 | async-start | bytes 4456448 | tf_op jit(solution)/shard_map/all_gather | solution.py:204
  9.1 111.4 %all-gather.8.cloned.1.call-start = ((), (), s32[]{:S(2)}) async-start(), calls=%async_computation.10 | async-start | bytes 5013504 | tf_op jit(solution)/shard_map/all_gather | solution.py:41
  39.5 19.5 %copy-start.30 = (bf16[2,2,1,128,256]{4,3,2,1,0:T(8,128)(2,1)S(1)}, bf16[2,2,1,128,256]{4,3,2,1,0:T(8,128)(2,1)}, u32[]{:S(2)}) copy-start(bf16[2,2,1,128,256]{4,3,2,1,0:T(8,128)(2,1)} %param.17) | copy-start | bytes 786436
  56.0 25.1 %copy-start.5 = (bf16[2,2,1,128,1024]{4,3,2,1,0:T(8,128)(2,1)S(1)}, bf16[2,2,1,128,1024]{4,3,2,1,0:T(8,128)(2,1)}, u32[]{:S(2)}) copy-start(bf16[2,2,1,128,1024]{4,3,2,1,0:T(8,128)(2,1)} %param.15) | copy-start | bytes 3145732
  58.9 216.6 %reduce-scatter.5.cloned.1.call-start = ((), (), s32[]{:S(2)}) async-start(), calls=%async_computation.8 | async-start | bytes 5013504 | tf_op jit(solution)/shard_map/reduce_scatter | solution.py:67
  59.1 38.4 %copy-start.38 = (bf16[1,1,1,128,256]{3,4,2,1,0:T(8,128)(2,1)}, bf16[1,1,1,128,256]{3,4,2,1,0:T(8,128)(2,1)S(1)}, u32[]{:S(2)}) copy-start(bf16[1,1,1,128,256]{3,4,2,1,0:T(8,128)(2,1)S(1)} %copy.477) | copy-start | bytes 196612
  59.2 32.9 %copy-start.42 = (bf16[1,1,1,128,256]{3,4,2,1,0:T(8,128)(2,1)}, bf16[1,1,1,128,256]{3,4,2,1,0:T(8,128)(2,1)S(1)}, u32[]{:S(2)}) copy-start(bf16[1,1,1,128,256]{3,4,2,1,0:T(8,128)(2,1)S(1)} %copy.475) | copy-start | bytes 196612
  59.4 30.1 %copy-start.40 = (bf16[1,1,1,128,256]{3,4,2,1,0:T(8,128)(2,1)}, bf16[1,1,1,128,256]{3,4,2,1,0:T(8,128)(2,1)S(1)}, u32[]{:S(2)}) copy-start(bf16[1,1,1,128,256]{3,4,2,1,0:T(8,128)(2,1)S(1)} %copy.473) | copy-start | bytes 196612
  59.5 45.4 %copy-start.41 = (bf16[1,1,1,128,256]{3,4,2,1,0:T(8,128)(2,1)}, bf16[1,1,1,128,256]{3,4,2,1,0:T(8,128)(2,1)S(1)}, u32[]{:S(2)}) copy-start(bf16[1,1,1,128,256]{3,4,2,1,0:T(8,128)(2,1)S(1)} %copy.471) | copy-start | bytes 196612
  90.0 10.2 %copy-start.17 = (f32[2,8,128,128]{2,3,1,0:T(8,128)}, f32[2,8,128,128]{2,3,1,0:T(8,128)S(1)}, u32[]{:S(2)}) copy-start(f32[2,8,128,128]{2,3,1,0:T(8,128)S(1)} %get-tuple-element.74) | copy-start | bytes 3145732
  97.6 10.5 %copy-start.3 = (bf16[2,1,128,1024]{3,2,1,0:T(8,128)(2,1)S(1)}, bf16[2,1,128,1024]{3,2,1,0:T(8,128)(2,1)}, u32[]{:S(2)}) copy-start(bf16[2,1,128,1024]{3,2,1,0:T(8,128)(2,1)} %param.18) | copy-start | bytes 1572868
  100.2 12.3 %copy-start.47 = (f32[2,8,128]{2,1,0:T(8,128)}, f32[2,8,128]{2,1,0:T(8,128)S(1)}, u32[]{:S(2)}) copy-start(f32[2,8,128]{2,1,0:T(8,128)S(1)} %get-tuple-element.75) | copy-start | bytes 24580
  116.4 45.2 %collective-permute-start = (bf16[128,1024]{1,0:T(8,128)(2,1)S(1)}, bf16[128,1024]{1,0:T(8,128)(2,1)}, u32[]{:S(2)}, u32[]{:S(2)}) collective-permute-start(bf16[128,1024]{1,0:T(8,128)(2,1)S(1)} %fusion.61), channel_id=1, source_target_pairs={{16,0},{32,16},{48,32},{64,48},{80,64},{96,80},{112,96},{128,112},... | collective-permute-start | bytes 786440 | tf_op jit(solution)/shard_map/ppermute | solution.py:52
  149.8 11.9 %collective-permute-start.1 = (bf16[128,1024]{1,0:T(8,128)(2,1)S(1)}, bf16[128,1024]{1,0:T(8,128)(2,1)S(1)}, u32[]{:S(2)}, u32[]{:S(2)}) collective-permute-start(bf16[128,1024]{1,0:T(8,128)(2,1)S(1)} %fusion.62), channel_id=1, source_target_pairs={{0,16},{16,32},{32,48},{48,64},{64,80},{80,96},{96,112},{112,128},... | collective-permute-start | bytes 786440 | tf_op jit(solution)/shard_map/ppermute | solution.py:52
  200.4 150.2 %reduce-scatter.3.cloned.1.call-start = ((), (), s32[]{:S(2)}) async-start(), calls=%async_computation.7 | async-start | bytes 5013504 | tf_op jit(solution)/shard_map/reduce_scatter | solution.py:67
  274.4 14.0 %copy-start.15 = (bf16[1,128,2048]{2,1,0:T(8,128)(2,1)S(1)}, bf16[1,128,2048]{2,1,0:T(8,128)(2,1)}, u32[]{:S(2)}) copy-start(bf16[1,128,2048]{2,1,0:T(8,128)(2,1)} %copy.383) | copy-start | bytes 1572868
  274.5 14.0 %copy-start.16 = (bf16[1,128,2048]{2,1,0:T(8,128)(2,1)S(1)}, bf16[1,128,2048]{2,1,0:T(8,128)(2,1)}, u32[]{:S(2)}) copy-start(bf16[1,128,2048]{2,1,0:T(8,128)(2,1)} %copy.376) | copy-start | bytes 1572868
  280.4 19.5 %all-to-all-start.2 = ((bf16[16,2,4608]{2,1,0:T(2,128)(2,1)}), bf16[16,2,4608]{2,1,0:T(2,128)(2,1)S(1)}, u32[]{:S(2)}, u32[]{:S(2)}) async-start(bf16[16,2,4608]{2,1,0:T(2,128)(2,1)} %reshape.462), calls=%async_computation.4 | async-start | bytes 589824 | tf_op jit(solution)/shard_map/all_to_all | solution.py:24
  290.1 73.7 %copy-start.31 = (f32[1,64,256]{2,1,0:T(8,128)S(1)}, f32[1,64,256]{2,1,0:T(8,128)}, u32[]{:S(2)}) copy-start(f32[1,64,256]{2,1,0:T(8,128)} %param.11) | copy-start | bytes 196612
  290.1 73.7 %copy-start.44 = (f32[1,64,256]{2,1,0:T(8,128)S(1)}, f32[1,64,256]{2,1,0:T(8,128)}, u32[]{:S(2)}) copy-start(f32[1,64,256]{2,1,0:T(8,128)} %param.13) | copy-start | bytes 196612
  300.6 72.9 %copy-start.14 = (f32[1,128,1024]{2,1,0:T(8,128)S(1)}, f32[1,128,1024]{2,1,0:T(8,128)}, u32[]{:S(2)}) copy-start(f32[1,128,1024]{2,1,0:T(8,128)} %param.12) | copy-start | bytes 1572868
  300.6 72.9 %copy-start.27 = (f32[1,128,1024]{2,1,0:T(8,128)S(1)}, f32[1,128,1024]{2,1,0:T(8,128)}, u32[]{:S(2)}) copy-start(f32[1,128,1024]{2,1,0:T(8,128)} %param.14) | copy-start | bytes 1572868
  301.4 51.7 %all-to-all-start.3 = ((bf16[16,2,512]{2,1,0:T(2,128)(2,1)}), bf16[16,2,512]{2,1,0:T(2,128)(2,1)S(1)}, u32[]{:S(2)}, u32[]{:S(2)}) async-start(bf16[16,2,512]{2,1,0:T(2,128)(2,1)} %reshape.464), calls=%async_computation.5 | async-start | bytes 65536 | tf_op jit(solution)/shard_map/all_to_all | solution.py:174
  353.1 20.2 %all-to-all-start.4 = ((bf16[16,128,64]{1,2,0:T(8,128)(2,1)}), bf16[16,128,64]{1,2,0:T(8,128)(2,1)S(1)}, u32[]{:S(2)}, u32[]{:S(2)}) async-start(bf16[16,128,64]{1,2,0:T(8,128)(2,1)} %rev.18), calls=%async_computation.6 | async-start | bytes 524288 | tf_op jit(solution)/shard_map/all_to_all | solution.py:177
  (40 other events, 212.5 us)
Sparse Core Ops, SparseCore 0:
  10.3 53.1 all-gather.5
  65.4 42.2 all-gather.7
  200.5 71.6 reduce-scatter.4
  274.6 75.9 reduce-scatter.2
where the time goes:
time: 389 us; the launch traced here: 382 us
  matrix products  98.3 us (25%)
  local copies, waits for them, and re-layouts  85.3 us (22%)
  waiting for transfers between devices  63 us (16%)
  blocking collectives  60.7 us (16%)
  starting transfers between devices  29.4 us (8%)
  other arithmetic  27.2 us (7%)
  between operations  17.6 us (5%)
    reduce_scatter x2, waiting for transfers between devices, sum_together(): lax.psum_scatter(lines, axis, tiled=True).reshape(-1)  44.4 us
    all_to_all x2, blocking collectives, side_by_side(): lax.all_to_all(both, axis, split_axis=split_dim, concat_axis=concat_dim,...  39.2 us
    dot_general x4, matrix products, backward(): jnp.einsum('tc,td->cd', attended, cotangent, preferred_element_type=jnp.f...  23.2 us
    all_gather x1, blocking collectives, shards(): lax.all_gather(own_value, 'lane', axis=0, tiled=True)  21.6 us
    dot_general x4, matrix products, backward(): jnp.einsum('hgij,jhd->ihgd', grad_scores, heads_of_key, preferred_element...  14.4 us
    dot_general x4, matrix products, backward(): jnp.einsum('hgij,ihgd->jhd', grad_scores, heads_of_query, preferred_eleme...  13.8 us
    unnamed x132, local copies, waits for them, and re-layouts  13.7 us
    another operation x4, local copies, waits for them, and re-layouts, sum_together(): lines = jnp.concatenate([b.reshape(size, -1) for b in tiles], axis=1)  12.2 us
  transfers between devices with their start and end apart: 9, of which 3 were waited for; matrix products, arithmetic and copies ran while one was open for 44% of the time, Pallas kernels for 0%

commit v1 on v0

v1 whole, which is shorter than its diff:
```python
import functools
import math

import jax
import jax.numpy as jnp
from jax import lax
from jax.experimental import pallas as pl
from jax.experimental.pallas import tpu as pltpu
from jax.sharding import PartitionSpec as P

TOK = 128
D = 1024
QW = 2048
KVW = 256
HS = 128
HEADS = 16
GROUP = 8
LANES = 16
ROWS = 144
CUT = 80

decay_rate = 0.9
learn_rate = 0.01
MESH = pl.DeviceIdType.MESH
bf16 = jnp.bfloat16
f32 = jnp.float32

PLACES = ((2, 1), (1, 1), (3, 1), (2, 0), (1, 0), (3, 0), (0, 1), (0, 0))


def dot(a, b, dims):
    return lax.dot_general(a, b, (dims, ((), ())), preferred_element_type=f32)


def kernel(
    sections,
    bn, bw, wv_in, wo_in, x_hbm, q_hbm, k_hbm, gnow_hbm, gnew_hbm,
    gi_hbm, dq_hbm, dk_hbm, gsum_ref,
    wb, wvs, xs, qs, ks, gs, gnews, pr, vs, at, ga, dvs, gis, dqs, dks, rx,
    dwv, pc, po, rc, rn, msend, mrecv, fin, maskb,
    ld_sem, st_sem, ag_send, ag_recv, rs_send, rs_recv, ms_send, ms_recv, nb_send, nb_recv,
):
    s = lax.axis_index("section")
    l = lax.axis_index("lane")
    y = l // 4
    x = (l // 2) % 2
    c = l % 2
    scale = 1.0 / math.sqrt(HS)

    def lane(dy, dx, dc):
        yy = (y + dy) % 4
        xx = (x + dx) % 2
        cc = (c + dc) % 2
        return yy * 4 + xx * 2 + cc

    def slot(q, dy, dx, dc):
        return lane(dy, dx + q, dc)

    xp = (s, lane(0, 1, 0))
    yp = (s, lane(1, 0, 0))
    ym = (s, lane(3, 0, 0))
    cp = (s, lane(0, 0, 1))
    mir = (sections - 1 - s, lane(0, 1, 0))
    before = ((s + sections - 1) % sections, l)
    after = ((s + 1) % sections, l)

    loads = [
        pltpu.make_async_copy(k_hbm, ks, ld_sem.at[0]),
        pltpu.make_async_copy(q_hbm, qs, ld_sem.at[1]),
        pltpu.make_async_copy(x_hbm, xs, ld_sem.at[2]),
        pltpu.make_async_copy(gnow_hbm, gs.at[:, 0], ld_sem.at[3]),
        pltpu.make_async_copy(gnew_hbm, gnews, ld_sem.at[4]),
    ]
    for cpy in loads:
        cpy.start()

    barrier = pltpu.get_barrier_semaphore()
    peers = (xp, yp, ym, cp, mir, before, after)
    for p in peers:
        pl.semaphore_signal(barrier, inc=1, device_id=p, device_id_type=MESH)
    wb[0, l, :TOK, :] = wo_in[...].astype(bf16)
    for j in range(4):
        wb[0, l, TOK:, j * KVW : (j + 1) * KVW] = wv_in[16 * j : 16 * (j + 1), :].astype(bf16)
    pl.semaphore_wait(barrier, len(peers))

    sent = []

    def send(src, dst, ssem, rsem, dev):
        cpy = pltpu.make_async_remote_copy(
            src_ref=src, dst_ref=dst, send_sem=ssem, recv_sem=rsem, device_id=dev, device_id_type=MESH
        )
        cpy.start()
        sent.append(cpy)

    def arrived(dst, sem):
        pltpu.make_async_copy(dst, dst, sem).wait()

    OWN, X, A, B, OPP, AX, BX, OX = range(8)
    where_is = {
        OWN: (0, 0), X: (0, 1), A: (3, 0), B: (1, 0), OPP: (2, 0), AX: (3, 1), BX: (1, 1), OX: (2, 1),
    }

    def block(q, kind, core=0):
        return wb.at[q, slot(q, *where_is[kind], core)]

    def ag_send_block(q, n, kind, to, rkind, rows=None):
        ref = block(q, kind)
        if rows is not None:
            ref = ref.at[pl.ds(*rows), :]
        send(ref, ref, ag_send.at[q, n], ag_recv.at[q, rkind], to)

    def ag_core(q, kind):
        ref = block(q, kind)
        send(ref, ref, ag_send.at[q, 8 + kind], ag_recv.at[q, 8 + kind], cp)

    def ag_start(q):
        ag_send_block(q, 0, OWN, yp, 1)
        ag_send_block(q, 1, OWN, ym, 2)
        ag_send_block(q, 2, OWN, xp, 0)
        ag_core(q, OWN)

    def ag_step1(q):
        arrived(block(q, A), ag_recv.at[q, 1])
        ag_send_block(q, 3, A, yp, 3, (0, CUT))
        arrived(block(q, B), ag_recv.at[q, 2])
        ag_send_block(q, 4, B, ym, 4, (CUT, ROWS - CUT))
        arrived(block(q, X), ag_recv.at[q, 0])
        ag_send_block(q, 5, X, yp, 5)
        ag_send_block(q, 6, X, ym, 6)
        ag_core(q, A)
        ag_core(q, B)
        ag_core(q, X)

    def ag_step2(q):
        ref = block(q, OPP)
        arrived(ref.at[pl.ds(0, CUT), :], ag_recv.at[q, 3])
        arrived(ref.at[pl.ds(CUT, ROWS - CUT), :], ag_recv.at[q, 4])
        ag_send_block(q, 7, OPP, xp, 7)
        ag_core(q, OPP)

    def ag_step3(q):
        arrived(block(q, AX), ag_recv.at[q, 5])
        ag_core(q, AX)
        arrived(block(q, BX), ag_recv.at[q, 6])
        ag_core(q, BX)
        arrived(block(q, OX), ag_recv.at[q, 7])
        ag_core(q, OX)

    def ag_finish(q):
        for kind in range(8):
            arrived(block(q, kind, 1), ag_recv.at[q, 8 + kind])

        @pl.loop(0, LANES)
        def _(h):
            for j in range(4):
                at_row = pl.multiple_of(h * 64 + 16 * j, 16)
                wvs[q, pl.ds(at_row, 16), :] = wb[q, h, TOK:, j * KVW : (j + 1) * KVW]

    def softmax(q, t):
        here = bn[q, s]
        if t == 0:
            bound = here
        elif q == 0:
            bound = jnp.where(s == sections - 1, bw[0], bn[0, jnp.minimum(s + 1, sections - 1)])
        else:
            bound = jnp.where(s == 0, bw[1], bn[1, jnp.maximum(s - 1, 0)])
        row = lax.broadcasted_iota(jnp.int32, (TOK, TOK), 0)
        col = lax.broadcasted_iota(jnp.int32, (TOK, TOK), 1)
        seen = (col <= row) & ((col >= bound) | (row < bound))
        maskb[...] = jnp.where(seen, 0.0, -1e30).astype(f32)
        for g in range(2):
            kg = ks[q, t, :, g * HS : (g + 1) * HS]

            @pl.loop(0, GROUP // 2)
            def _(n):
                for u in range(2):
                    h = g * GROUP + n * 2 + u
                    qh = qs[q, t, :, pl.ds(pl.multiple_of(h * HS, HS), HS)]
                    sc = dot(qh, kg, ((1,), (1,))) * scale + maskb[...]
                    e = jnp.exp(sc - jnp.max(sc, axis=-1, keepdims=True))
                    pr[q, t, h] = e * (1.0 / jnp.sum(e, axis=-1, keepdims=True))

    def values(q):
        for t in range(2):
            vs[q, t] = dot(xs[q, t], wvs[q], ((1,), (0,))).astype(bf16)

    def attended(q, t):
        for g in range(2):
            vg = vs[q, t, :, g * HS : (g + 1) * HS]

            @pl.loop(0, GROUP // 2)
            def _(n):
                for u in range(2):
                    h = g * GROUP + n * 2 + u
                    at[q, h, t * TOK : (t + 1) * TOK, :] = dot(pr[q, t, h].astype(bf16), vg, ((1,), (0,))).astype(bf16)

    def tick(q, t):
        @pl.loop(0, HEADS // 2)
        def _(n):
            w2 = jnp.concatenate([wb[q, 2 * n, :TOK, :], wb[q, 2 * n + 1, :TOK, :]], axis=0)
            r = dot(gs[q, t], w2, ((1,), (1,))).astype(bf16)
            ga[q, t, 2 * n] = r[:, :HS]
            ga[q, t, 2 * n + 1] = r[:, HS:]

        for g in range(2):
            p8 = pr[q, t, g * GROUP : (g + 1) * GROUP].astype(bf16).reshape(GROUP * TOK, TOK)
            g8 = ga[q, t, g * GROUP : (g + 1) * GROUP].reshape(GROUP * TOK, HS)
            dvs[q, t, :, g * HS : (g + 1) * HS] = dot(p8, g8, ((0,), (0,))).astype(bf16)
        for n in range(4):
            cols = slice(n * 256, (n + 1) * 256)
            add = dot(dvs[q, t], wvs[q, cols, :], ((1,), (1,)))
            gis[q, t, :, cols] = (gs[q, t, :, cols].astype(f32) + add).astype(bf16)

    def send_on(q):
        send(gis.at[q, 0], rx.at[q], nb_send.at[q], nb_recv.at[q], before if q == 0 else after)

    def take(q):
        arrived(rx.at[q], nb_recv.at[q])
        at_end = s == (sections - 1 if q == 0 else 0)
        gs[q, 1] = jnp.where(at_end, gnews[q], rx[q])

    def score_grads(q, t):
        for g in range(2):
            kg = ks[q, t, :, g * HS : (g + 1) * HS]
            vg = vs[q, t, :, g * HS : (g + 1) * HS]

            def body(n, acc):
                for u in range(2):
                    h = g * GROUP + n * 2 + u
                    at_col = pl.ds(pl.multiple_of(h * HS, HS), HS)
                    gp = dot(ga[q, t, h], vg, ((1,), (1,)))
                    p = pr[q, t, h]
                    delta = jnp.sum(p * gp, axis=-1, keepdims=True)
                    ds = (p * (gp - delta) * scale).astype(bf16)
                    dqs[q, t, :, at_col] = dot(ds, kg, ((1,), (0,))).astype(bf16)
                    acc = acc + dot(ds, qs[q, t, :, at_col], ((0,), (0,)))
                return acc

            acc = lax.fori_loop(0, GROUP // 2, body, jnp.zeros((TOK, HS), f32))
            dks[q, t, :, g * HS : (g + 1) * HS] = acc.astype(bf16)

    stores = []

    def store(src, dst):
        cpy = pltpu.make_async_copy(src, dst, st_sem.at[len(stores)])
        cpy.start()
        stores.append(cpy)

    def store_scores(q, t):
        store(dqs.at[q, t], dq_hbm.at[q, t])
        store(dks.at[q, t], dk_hbm.at[q, t])

    def rs_partials(q):
        xt = xs[q].reshape(2 * TOK, D)
        dv = dvs[q].reshape(2 * TOK, KVW)
        for n in range(4):
            dwv[q, n * 256 : (n + 1) * 256, :] = dot(xt[:, n * 256 : (n + 1) * 256], dv, ((0,), (0,))).astype(bf16)

        def one(ref, i, dc):
            dy, dx = PLACES[i]
            r = slot(q, dy, dx, dc)
            a = at[q, r]
            for n in range(2):
                cols = slice(n * 512, (n + 1) * 512)
                gg = gs[q, :, :, cols].reshape(2 * TOK, 512)
                ref[q, i, :TOK, cols] = dot(a, gg, ((0,), (0,))).astype(bf16)
            for j in range(4):
                at_row = pl.multiple_of(r * 64 + 16 * j, 16)
                ref[q, i, TOK:, j * KVW : (j + 1) * KVW] = dwv[q, pl.ds(at_row, 16), :]

        for i in range(8):
            one(pc, i, 1)
            send(pc.at[q, i], rc.at[q, i], rs_send.at[q, 8 + i], rs_recv.at[q, 8 + i], cp)
        for i in range(8):
            one(po, i, 0)

    R1, R2A, R2B, R3A, R3B, R4A, R4B, R5 = range(8)

    def plus(q, i, more, rows=slice(None)):
        total = po[q, i, rows, :].astype(f32)
        for n in more:
            total = total + (rn[q, n, rows, :] if n < 8 else rc[q, n - 8, rows, :]).astype(f32)
        return total

    def add_in(q, i, more, rows=slice(None)):
        po[q, i, rows, :] = plus(q, i, more, rows).astype(bf16)

    def rs_core(q, i):
        arrived(rc.at[q, i], rs_recv.at[q, 8 + i])

    def rs_hop(q, n, i, to, rows=None):
        src, dst = po.at[q, i], rn.at[q, n]
        if rows is not None:
            src, dst = src.at[pl.ds(*rows), :], dst.at[pl.ds(*rows), :]
        send(src, dst, rs_send.at[q, n], rs_recv.at[q, n], to)

    def rs_got(q, n, rows=None):
        dst = rn.at[q, n]
        if rows is not None:
            dst = dst.at[pl.ds(*rows), :]
        arrived(dst, rs_recv.at[q, n])

    def rs_a(q):
        for i, n, to in ((0, R1, xp), (1, R2A, yp), (2, R2B, ym)):
            rs_core(q, i)
            add_in(q, i, (8 + i,))
            rs_hop(q, n, i, to)

    def rs_b(q):
        rs_core(q, 3)
        rs_got(q, R1)
        add_in(q, 3, (8 + 3, R1))
        rs_hop(q, R3A, 3, yp, (0, CUT))
        rs_hop(q, R3B, 3, ym, (CUT, ROWS - CUT))
        rs_core(q, 6)
        rs_got(q, R2A)
        rs_got(q, R2B)
        add_in(q, 6, (8 + 6, R2A, R2B))
        rs_hop(q, R5, 6, xp)

    def rs_c(q):
        rs_core(q, 4)
        rs_got(q, R3A, (0, CUT))
        add_in(q, 4, (8 + 4, R3A), slice(0, CUT))
        add_in(q, 4, (8 + 4,), slice(CUT, ROWS))
        rs_hop(q, R4A, 4, yp)
        rs_core(q, 5)
        rs_got(q, R3B, (CUT, ROWS - CUT))
        add_in(q, 5, (8 + 5, R3B), slice(CUT, ROWS))
        add_in(q, 5, (8 + 5,), slice(0, CUT))
        rs_hop(q, R4B, 5, ym)

    def rs_final(q):
        rs_core(q, 7)
        rs_got(q, R4A)
        rs_got(q, R4B)
        rs_got(q, R5)
        total = plus(q, 7, (8 + 7, R4A, R4B, R5))
        if q == 0:
            fin[...] = total
        else:
            msend[...] = total.astype(bf16)
            send(msend, mrecv, ms_send.at[1], ms_recv.at[1], mir)

    own = block(0, OWN)
    send(own, wb.at[1, l], ms_send.at[0], ms_recv.at[0], mir)
    ag_start(0)
    loads[0].wait()
    loads[1].wait()
    softmax(0, 0)
    ag_step1(0)
    softmax(0, 1)
    ag_step2(0)
    softmax(1, 0)
    arrived(block(1, OWN), ms_recv.at[0])
    ag_start(1)
    ag_step3(0)
    loads[2].wait()
    loads[3].wait()
    loads[4].wait()
    ag_finish(0)
    values(0)
    tick(0, 0)
    send_on(0)
    store(gis.at[0, 0], gi_hbm.at[0, 0])
    ag_step1(1)
    attended(0, 0)
    attended(0, 1)
    ag_step2(1)
    softmax(1, 1)
    take(0)
    tick(0, 1)
    store(gis.at[0, 1], gi_hbm.at[0, 1])
    ag_step3(1)
    rs_partials(0)
    ag_finish(1)
    values(1)
    tick(1, 0)
    send_on(1)
    store(gis.at[1, 0], gi_hbm.at[1, 0])
    rs_a(0)
    attended(1, 0)
    attended(1, 1)
    rs_b(0)
    take(1)
    tick(1, 1)
    store(gis.at[1, 1], gi_hbm.at[1, 1])
    rs_c(0)
    rs_partials(1)
    rs_a(1)
    rs_final(0)
    score_grads(1, 0)
    store_scores(1, 0)
    rs_b(1)
    score_grads(1, 1)
    store_scores(1, 1)
    rs_c(1)
    score_grads(0, 0)
    store_scores(0, 0)
    rs_final(1)
    score_grads(0, 1)
    store_scores(0, 1)
    arrived(mrecv, ms_recv.at[1])
    gsum_ref[...] = (fin[...] + mrecv[...].astype(f32)) / LANES
    for cpy in stores:
        cpy.wait()
    for cpy in sent:
        cpy.wait_send()


def shards(
    value_weight, out_weight, value_moment, out_moment, inputs_saved, queries_saved, keys_saved,
    grad_now, grad_new, bound_now, bound_new,
):
    sections = lax.axis_size("section")
    hbm = pl.BlockSpec(memory_space=pl.ANY)
    vmem = pl.BlockSpec(memory_space=pltpu.VMEM)
    smem = pl.BlockSpec(memory_space=pltpu.SMEM)
    dma = pltpu.SemaphoreType.DMA
    gi, dq, dk, gsum = pl.pallas_call(
        functools.partial(kernel, sections),
        out_shape=(
            jax.ShapeDtypeStruct((2, 2, TOK, D), bf16),
            jax.ShapeDtypeStruct((2, 2, TOK, QW), bf16),
            jax.ShapeDtypeStruct((2, 2, TOK, KVW), bf16),
            jax.ShapeDtypeStruct((ROWS, D), f32),
        ),
        in_specs=[smem, smem, vmem, vmem, hbm, hbm, hbm, hbm, hbm],
        out_specs=(hbm, hbm, hbm, vmem),
        scratch_shapes=[
            pltpu.VMEM((2, LANES, ROWS, D), bf16),
            pltpu.VMEM((2, D, KVW), bf16),
            pltpu.VMEM((2, 2, TOK, D), bf16),
            pltpu.VMEM((2, 2, TOK, QW), bf16),
            pltpu.VMEM((2, 2, TOK, KVW), bf16),
            pltpu.VMEM((2, 2, TOK, D), bf16),
            pltpu.VMEM((2, TOK, D), bf16),
            pltpu.VMEM((2, 2, HEADS, TOK, TOK), f32),
            pltpu.VMEM((2, 2, TOK, KVW), bf16),
            pltpu.VMEM((2, HEADS, 2 * TOK, HS), bf16),
            pltpu.VMEM((2, 2, HEADS, TOK, HS), bf16),
            pltpu.VMEM((2, 2, TOK, KVW), bf16),
            pltpu.VMEM((2, 2, TOK, D), bf16),
            pltpu.VMEM((2, 2, TOK, QW), bf16),
            pltpu.VMEM((2, 2, TOK, KVW), bf16),
            pltpu.VMEM((2, TOK, D), bf16),
            pltpu.VMEM((2, D, KVW), bf16),
            pltpu.VMEM((2, 8, ROWS, D), bf16),
            pltpu.VMEM((2, 8, ROWS, D), bf16),
            pltpu.VMEM((2, 8, ROWS, D), bf16),
            pltpu.VMEM((2, 8, ROWS, D), bf16),
            pltpu.VMEM((ROWS, D), bf16),
            pltpu.VMEM((ROWS, D), bf16),
            pltpu.VMEM((ROWS, D), f32),
            pltpu.VMEM((TOK, TOK), f32),
            dma((5,)),
            dma((12,)),
            dma((2, 16)),
            dma((2, 16)),
            dma((2, 16)),
            dma((2, 16)),
            dma((2,)),
            dma((2,)),
            dma((2,)),
            dma((2,)),
        ],
        compiler_params=pltpu.CompilerParams(
            collective_id=0, has_side_effects=True, vmem_limit_bytes=64000 * 1024
        ),
    )(
        bound_now[:, :, 0], bound_new[:, 0], value_weight[0], out_weight[0],
        inputs_saved[:, :, 0], queries_saved[:, :, 0], keys_saved[:, :, 0], grad_now[:, 0], grad_new,
    )
    mean_out = gsum[:TOK]
    tail = gsum[TOK:]
    mean_value = jnp.concatenate([tail[:, j * KVW : (j + 1) * KVW] for j in range(4)], axis=0)
    value_moment_new = decay_rate * value_moment + mean_value[None]
    out_moment_new = decay_rate * out_moment + mean_out[None]
    value_weight_new = value_weight - learn_rate * value_moment_new
    out_weight_new = out_weight - learn_rate * out_moment_new
    return (
        gi[:, :, None], dq[:, :, None], dk[:, :, None],
        value_weight_new, out_weight_new, value_moment_new, out_moment_new,
    )


def solution(mesh):
    return jax.shard_map(
        shards,
        mesh=mesh,
        in_specs=(
            P("section", "lane", None),
            P("section", "lane", None),
            P("section", "lane", None),
            P("section", "lane", None),
            P(None, None, "section", "lane", None),
            P(None, None, "section", "lane", None),
            P(None, None, "section", "lane", None),
            P(None, "section", "lane", None),
            P(None, "lane", None),
            P(None, None, "lane"),
            P(None, "lane"),
        ),
        out_specs=(
            P(None, None, "section", "lane", None),
            P(None, None, "section", "lane", None),
            P(None, None, "section", "lane", None),
            P("section", "lane", None),
            P("section", "lane", None),
            P("section", "lane", None),
            P("section", "lane", None),
        ),
        check_vma=False,
    )
```

time: 389 us -> 120 us (0.31)
  the two profiles are of different devices: /device:TPU:32 before, /device:TPU:1 now
where the time goes in v1:
time: 120 us
  Pallas kernels  112 us (93%)
  local copies, waits for them, and re-layouts  3.88 us (3%)
  other arithmetic  3.01 us (3%)
    pallas_call x1, Pallas kernels, shards(): pl.pallas_call(functools.partial(kernel, sections), out_shape=(jax.ShapeD...  112 us
    unnamed x17, local copies, waits for them, and re-layouts  3.02 us

profile of v1, /device:TPU:1, one launch (start us, length us, event | category | flops | bytes accessed | tf_op | source)
XLA Modules:
  0.0 119.7 jit_solution(10696560922105703453)
XLA Ops:
  0.6 0.0 copy-start.4
  0.6 0.0 copy-start.6
  0.7 0.0 copy-start
  0.7 0.0 copy-start.3
  0.7 112.1 %shard_map.162 = (bf16[2,2,128,1024]{3,2,1,0:T(8,128)(2,1)}, bf16[2,2,128,2048]{3,2,1,0:T(8,128)(2,1)}, bf16[2,2,128,256]{3,2,1,0:T(8,128)(2,1)}, f32[144,1024]{1,0:T(8,128)}) custom-call(s32[2,16]{1,0:T(2,128)} %bitcast.34, s32[2]{0:T(128)} %bitcast.35, f32[64,256]{1,0:T(8,128)} %bitcast.31, f32[128,1024]{1,0:T(8,128)} %bitcast.25, ...), custom_call_target="tpu_custom_call" | custom-call | tf_op jit(solution)/shard_map/pallas_call | solution.py:420
  112.8 0.0 copy-start.2
  112.8 0.9 fusion.2
  113.7 0.0 copy-done.4
  113.7 0.0 copy-done.6
  113.7 0.7 multiply_subtract_fusion.1
  114.3 0.0 copy-done
  114.3 0.0 copy-done.3
  114.4 0.0 copy-start.1
  114.4 2.3 %multiply_subtract_fusion = (f32[1,128,1024]{2,1,0:T(8,128)}, f32[1,128,1024]{2,1,0:T(8,128)}) fusion(f32[1,128,1024]{2,1,0:T(8,128)S(1)} %copy-done, f32[144,1024]{1,0:T(8,128)} %get-tuple-element.14, f32[1,128,1024]{2,1,0:T(8,128)S(1)} %copy-done.3), kind=kLoop, calls=%fused_computation.1 | loop fusion | flops 524288 | bytes 2621440 | tf_op jit(solution)/shard_map/sub | solution.py:480
  116.7 0.0 copy-done.2
  116.7 1.0 copy.24
  117.7 0.0 copy-done.1
  117.7 0.0 copy-start.5
  117.7 1.3 %copy.25 = bf16[2,2,1,128,2048]{4,3,2,1,0:T(8,128)(2,1)} copy(bf16[2,2,1,128,2048]{4,3,2,1,0:T(8,128)(2,1)S(1)} %bitcast.27) | data formatting | bytes 4194304
  119.0 0.0 copy-done.5
  119.0 0.7 copy.26
Async XLA Ops:
  0.6 113.0 %copy-start.4 = (f32[1,64,256]{2,1,0:T(8,128)S(1)}, f32[1,64,256]{2,1,0:T(8,128)}, u32[]{:S(2)}) copy-start(f32[1,64,256]{2,1,0:T(8,128)} %param.11) | copy-start | bytes 196612
  0.6 113.0 %copy-start.6 = (f32[1,64,256]{2,1,0:T(8,128)S(1)}, f32[1,64,256]{2,1,0:T(8,128)}, u32[]{:S(2)}) copy-start(f32[1,64,256]{2,1,0:T(8,128)} %param.13) | copy-start | bytes 196612
  0.7 113.7 %copy-start = (f32[1,128,1024]{2,1,0:T(8,128)S(1)}, f32[1,128,1024]{2,1,0:T(8,128)}, u32[]{:S(2)}) copy-start(f32[1,128,1024]{2,1,0:T(8,128)} %param.12) | copy-start | bytes 1572868
  0.7 113.7 %copy-start.3 = (f32[1,128,1024]{2,1,0:T(8,128)S(1)}, f32[1,128,1024]{2,1,0:T(8,128)}, u32[]{:S(2)}) copy-start(f32[1,128,1024]{2,1,0:T(8,128)} %param.14) | copy-start | bytes 1572868
  112.8 3.9 %copy-start.2 = (bf16[2,2,128,1024]{3,2,1,0:T(8,128)(2,1)S(1)}, bf16[2,2,128,1024]{3,2,1,0:T(8,128)(2,1)}, u32[]{:S(2)}) copy-start(bf16[2,2,128,1024]{3,2,1,0:T(8,128)(2,1)} %get-tuple-element.11) | copy-start | bytes 3145732
  114.4 3.3 %copy-start.1 = (bf16[2,2,128,2048]{3,2,1,0:T(8,128)(2,1)S(1)}, bf16[2,2,128,2048]{3,2,1,0:T(8,128)(2,1)}, u32[]{:S(2)}) copy-start(bf16[2,2,128,2048]{3,2,1,0:T(8,128)(2,1)} %get-tuple-element.12) | copy-start | bytes 6291460
  117.7 1.3 %copy-start.5 = (bf16[2,2,128,256]{3,2,1,0:T(8,128)(2,1)S(1)}, bf16[2,2,128,256]{3,2,1,0:T(8,128)(2,1)}, u32[]{:S(2)}) copy-start(bf16[2,2,128,256]{3,2,1,0:T(8,128)(2,1)} %get-tuple-element.13) | copy-start | bytes 786436

commit v2 on v1

v2 whole, which is shorter than its diff:
```python
import functools
import math

import jax
import jax.numpy as jnp
from jax import lax
from jax.experimental import pallas as pl
from jax.experimental.pallas import tpu as pltpu
from jax.sharding import PartitionSpec as P

TOK = 128
D = 1024
QW = 2048
KVW = 256
HS = 128
HEADS = 16
GROUP = 8
LANES = 16
ROWS = 144
CUT = 80
VROWS = 16
HALF = TOK // 2
WIDE = D // 2

decay_rate = 0.9
learn_rate = 0.01
MESH = pl.DeviceIdType.MESH
bf16 = jnp.bfloat16
f32 = jnp.float32

PLACES = ((2, 1), (1, 1), (3, 1), (2, 0), (1, 0), (3, 0), (0, 1), (0, 0))


def dot(a, b, dims):
    return lax.dot_general(a, b, (dims, ((), ())), preferred_element_type=f32)


def kernel(
    sections,
    bn, bw, wv_in, wo_in, x_hbm, q_hbm, k_hbm, gnow_hbm, gnew_hbm,
    gi_hbm, dq_hbm, dk_hbm, fo_hbm, fv_hbm, mo_hbm, mv_hbm,
    wb, wvs, xs, qs, ks, gs, gnews, pr, vs, at, ga, dvs, gis, dqs, dks, rx,
    dwv, pc, po, rc, rn, pcv, pov, rcv, rnv, msend, msendv, fin, finv, maskb,
    ld_sem, st_sem, ag_send, ag_recv, rs_send, rs_recv, rv_send, rv_recv, ms_send, ms_recv, nb_send, nb_recv,
):
    s = lax.axis_index("section")
    l = lax.axis_index("lane")
    y = l // 4
    x = (l // 2) % 2
    c = l % 2
    scale = 1.0 / math.sqrt(HS)

    def lane(dy, dx, dc):
        yy = (y + dy) % 4
        xx = (x + dx) % 2
        cc = (c + dc) % 2
        return yy * 4 + xx * 2 + cc

    def slot(q, dy, dx, dc):
        return lane(dy, dx + q, dc)

    xp = (s, lane(0, 1, 0))
    yp = (s, lane(1, 0, 0))
    ym = (s, lane(3, 0, 0))
    cp = (s, lane(0, 0, 1))
    mir = (sections - 1 - s, lane(0, 1, 0))
    before = ((s + sections - 1) % sections, l)
    after = ((s + 1) % sections, l)

    loads = [
        pltpu.make_async_copy(k_hbm, ks, ld_sem.at[0]),
        pltpu.make_async_copy(q_hbm, qs, ld_sem.at[1]),
        pltpu.make_async_copy(x_hbm, xs, ld_sem.at[2]),
        pltpu.make_async_copy(gnow_hbm, gs.at[:, 0], ld_sem.at[3]),
        pltpu.make_async_copy(gnew_hbm, gnews, ld_sem.at[4]),
    ]
    for cpy in loads:
        cpy.start()

    barrier = pltpu.get_barrier_semaphore()
    peers = (xp, yp, ym, cp, mir, before, after) + tuple((s, lane(dy, dx, 0)) for dy, dx in PLACES[:4])
    for p in peers:
        pl.semaphore_signal(barrier, inc=1, device_id=p, device_id_type=MESH)
    wb[0, l, :TOK, :] = wo_in[...].astype(bf16)
    for j in range(4):
        wb[0, l, TOK:, j * KVW : (j + 1) * KVW] = wv_in[16 * j : 16 * (j + 1), :].astype(bf16)
    pl.semaphore_wait(barrier, len(peers))

    sent = []

    def send(src, dst, ssem, rsem, dev):
        cpy = pltpu.make_async_remote_copy(
            src_ref=src, dst_ref=dst, send_sem=ssem, recv_sem=rsem, device_id=dev, device_id_type=MESH
        )
        cpy.start()
        sent.append(cpy)

    def arrived(dst, sem):
        pltpu.make_async_copy(dst, dst, sem).wait()

    OWN, X, A, B, OPP, AX, BX, OX = range(8)
    where_is = {
        OWN: (0, 0), X: (0, 1), A: (3, 0), B: (1, 0), OPP: (2, 0), AX: (3, 1), BX: (1, 1), OX: (2, 1),
    }

    def block(q, kind, core=0):
        return wb.at[q, slot(q, *where_is[kind], core)]

    def ag_send_block(q, n, kind, to, rkind, rows=None):
        ref = block(q, kind)
        if rows is not None:
            ref = ref.at[pl.ds(*rows), :]
        send(ref, ref, ag_send.at[q, n], ag_recv.at[q, rkind], to)

    def ag_core(q, kind):
        ref = block(q, kind)
        send(ref, ref, ag_send.at[q, 8 + kind], ag_recv.at[q, 8 + kind], cp)

    def ag_start(q):
        ag_send_block(q, 0, OWN, yp, 1, (0, CUT))
        ag_send_block(q, 1, OWN, ym, 2, (CUT, ROWS - CUT))
        ag_send_block(q, 2, OWN, xp, 0)
        ag_send_block(q, 16, OWN, yp, 16, (CUT, ROWS - CUT))
        ag_send_block(q, 17, OWN, ym, 17, (0, CUT))
        ag_core(q, OWN)

    def part(q, kind, first):
        return block(q, kind).at[pl.ds(*((0, CUT) if first else (CUT, ROWS - CUT))), :]

    def ag_step1(q):
        arrived(part(q, A, True), ag_recv.at[q, 1])
        ag_send_block(q, 3, A, yp, 3, (0, CUT))
        arrived(part(q, B, False), ag_recv.at[q, 2])
        ag_send_block(q, 4, B, ym, 4, (CUT, ROWS - CUT))

    def ag_step1b(q):
        arrived(block(q, X), ag_recv.at[q, 0])
        ag_send_block(q, 5, X, yp, 5)
        ag_send_block(q, 6, X, ym, 6)
        arrived(part(q, A, False), ag_recv.at[q, 16])
        ag_core(q, A)
        arrived(part(q, B, True), ag_recv.at[q, 17])
        ag_core(q, B)
        ag_core(q, X)

    def ag_step2(q):
        arrived(part(q, OPP, True), ag_recv.at[q, 3])
        arrived(part(q, OPP, False), ag_recv.at[q, 4])
        ag_send_block(q, 7, OPP, xp, 7)
        ag_core(q, OPP)

    def ag_step3(q):
        arrived(block(q, AX), ag_recv.at[q, 5])
        ag_core(q, AX)
        arrived(block(q, BX), ag_recv.at[q, 6])
        ag_core(q, BX)
        arrived(block(q, OX), ag_recv.at[q, 7])
        ag_core(q, OX)

    def grad_attended(q, kinds):
        for kind in kinds:
            arrived(block(q, kind, 1), ag_recv.at[q, 8 + kind])
            n = slot(q, *where_is[kind], 0) // 2
            w2 = jnp.concatenate([wb[q, 2 * n, :TOK, :], wb[q, 2 * n + 1, :TOK, :]], axis=0)
            r = dot(gs[q, 0], w2, ((1,), (1,))).astype(bf16)
            ga[q, 0, 2 * n] = r[:, :HS]
            ga[q, 0, 2 * n + 1] = r[:, HS:]

    def value_rows(q):
        @pl.loop(0, LANES)
        def _(h):
            for j in range(4):
                at_row = pl.multiple_of(h * 64 + 16 * j, 16)
                wvs[q, pl.ds(at_row, 16), :] = wb[q, h, TOK:, j * KVW : (j + 1) * KVW]

    stores = []

    def store(src, dst):
        cpy = pltpu.make_async_copy(src, dst, st_sem.at[len(stores)])
        cpy.start()
        stores.append(cpy)

    def softmax(q, t):
        here = bn[q, s]
        if t == 0:
            bound = here
        elif q == 0:
            bound = jnp.where(s == sections - 1, bw[0], bn[0, jnp.minimum(s + 1, sections - 1)])
        else:
            bound = jnp.where(s == 0, bw[1], bn[1, jnp.maximum(s - 1, 0)])
        row = lax.broadcasted_iota(jnp.int32, (TOK, TOK), 0)
        col = lax.broadcasted_iota(jnp.int32, (TOK, TOK), 1)
        seen = (col <= row) & ((col >= bound) | (row < bound))
        maskb[...] = jnp.where(seen, 0.0, -1e30).astype(f32)
        for g in range(2):
            kg = ks[q, t, :, g * HS : (g + 1) * HS]

            @pl.loop(0, GROUP // 2)
            def _(n):
                for u in range(2):
                    h = g * GROUP + n * 2 + u
                    qh = qs[q, t, :, pl.ds(pl.multiple_of(h * HS, HS), HS)]
                    sc = dot(qh, kg, ((1,), (1,))) * scale + maskb[...]
                    e = jnp.exp(sc - jnp.max(sc, axis=-1, keepdims=True))
                    pr[q, t, h] = e * (1.0 / jnp.sum(e, axis=-1, keepdims=True))

    def values(q):
        for t in range(2):
            vs[q, t] = dot(xs[q, t], wvs[q], ((1,), (0,))).astype(bf16)

    def attended(q, t):
        for g in range(2):
            vg = vs[q, t, :, g * HS : (g + 1) * HS]

            @pl.loop(0, GROUP // 2)
            def _(n):
                for u in range(2):
                    h = g * GROUP + n * 2 + u
                    at[q, h, t * TOK : (t + 1) * TOK, :] = dot(pr[q, t, h].astype(bf16), vg, ((1,), (0,))).astype(bf16)

    def grad_attended_late(q):
        @pl.loop(0, HEADS // 2)
        def _(n):
            w2 = jnp.concatenate([wb[q, 2 * n, :TOK, :], wb[q, 2 * n + 1, :TOK, :]], axis=0)
            r = dot(gs[q, 1], w2, ((1,), (1,))).astype(bf16)
            ga[q, 1, 2 * n] = r[:, :HS]
            ga[q, 1, 2 * n + 1] = r[:, HS:]

    def grad_values(q, t):
        for g in range(2):
            p8 = pr[q, t, g * GROUP : (g + 1) * GROUP].astype(bf16).reshape(GROUP * TOK, TOK)
            g8 = ga[q, t, g * GROUP : (g + 1) * GROUP].reshape(GROUP * TOK, HS)
            dvs[q, t, :, g * HS : (g + 1) * HS] = dot(p8, g8, ((0,), (0,))).astype(bf16)
        for n in range(4):
            cols = slice(n * 256, (n + 1) * 256)
            add = dot(dvs[q, t], wvs[q, cols, :], ((1,), (1,)))
            gis[q, t, :, cols] = (gs[q, t, :, cols].astype(f32) + add).astype(bf16)
            if t == 0 and n % 2:
                send(
                    gis.at[q, 0, :, pl.ds(n // 2 * WIDE, WIDE)], rx.at[q, n // 2],
                    nb_send.at[q, n // 2], nb_recv.at[q, n // 2], before if q == 0 else after,
                )
        store(gis.at[q, t], gi_hbm.at[q, t])

    def take(q, n):
        arrived(rx.at[q, n], nb_recv.at[q, n])
        at_end = s == (sections - 1 if q == 0 else 0)
        cols = slice(n * WIDE, (n + 1) * WIDE)
        gs[q, 1, :, cols] = jnp.where(at_end, gnews[q, :, cols], rx[q, n])

    def score_grads(q, t, only=None):
        for g in range(2) if only is None else (only,):
            kg = ks[q, t, :, g * HS : (g + 1) * HS]
            vg = vs[q, t, :, g * HS : (g + 1) * HS]

            def body(n, acc):
                for u in range(2):
                    h = g * GROUP + n * 2 + u
                    at_col = pl.ds(pl.multiple_of(h * HS, HS), HS)
                    gp = dot(ga[q, t, h], vg, ((1,), (1,)))
                    p = pr[q, t, h]
                    delta = jnp.sum(p * gp, axis=-1, keepdims=True)
                    ds = (p * (gp - delta) * scale).astype(bf16)
                    dqs[q, t, :, at_col] = dot(ds, kg, ((1,), (0,))).astype(bf16)
                    acc = acc + dot(ds, qs[q, t, :, at_col], ((0,), (0,)))
                return acc

            acc = lax.fori_loop(0, GROUP // 2, body, jnp.zeros((TOK, HS), f32))
            dks[q, t, :, g * HS : (g + 1) * HS] = acc.astype(bf16)

    def store_scores(q, t):
        store(dqs.at[q, t], dq_hbm.at[q, t])
        store(dks.at[q, t], dk_hbm.at[q, t])

    def rs_blocks(q, k, places=(0, 1, 2, 3, 4, 5, 6, 7)):
        def one(ref, i, dc):
            r = slot(q, *PLACES[i], dc)
            a = at[q, r]
            gg = gs[q, :, :, k * WIDE : (k + 1) * WIDE].reshape(2 * TOK, WIDE)
            ref[q, k, i] = dot(a, gg, ((0,), (0,))).astype(bf16)

        for i in places:
            one(pc, i, 1)
            send(pc.at[q, k, i], rc.at[q, k, i], rs_send.at[q, k, 11 + i], rs_recv.at[q, k, 11 + i], cp)
        for i in places:
            one(po, i, 0)

    R1A, R1B, R2A, R2B, R3A, R3B, R4AE, R4AL, R4BE, R4BL, R5 = range(11)
    UP, LOW, ALL = (0, HALF), (HALF, HALF), (0, TOK)
    PLACE_OF = {R1A: 0, R1B: 0, R2A: 1, R2B: 2, R3A: 3, R3B: 3, R4AE: 4, R4AL: 4, R4BE: 5, R4BL: 5, R5: 6}

    def rows_of(ref, rows):
        return ref.at[pl.ds(*rows), :]

    def rs_core(q, k, i):
        arrived(rc.at[q, k, i], rs_recv.at[q, k, 11 + i])

    def rs_hop(q, k, n, i, to, rows=ALL):
        send(
            rows_of(po.at[q, k, i], rows), rows_of(rn.at[q, k, PLACE_OF[n]], rows),
            rs_send.at[q, k, n], rs_recv.at[q, k, n], to,
        )

    def rs_got(q, k, n, rows=ALL):
        arrived(rows_of(rn.at[q, k, PLACE_OF[n]], rows), rs_recv.at[q, k, n])

    def add_in(q, k, i, more, rows=ALL, core=True):
        rr = slice(rows[0], rows[0] + rows[1])
        total = po[q, k, i, rr, :].astype(f32)
        if core:
            total = total + rc[q, k, i, rr, :].astype(f32)
        for n in more:
            total = total + rn[q, k, PLACE_OF[n], rr, :].astype(f32)
        return total

    def put(q, k, i, more, rows=ALL, core=True):
        po[q, k, i, rows[0] : rows[0] + rows[1], :] = add_in(q, k, i, more, rows, core).astype(bf16)

    def rs_a(q, k):
        rs_core(q, k, 0)
        put(q, k, 0, ())
        rs_hop(q, k, R1A, 0, xp, UP)
        rs_hop(q, k, R1B, 0, xp, LOW)
        rs_core(q, k, 1)
        put(q, k, 1, ())
        rs_hop(q, k, R2A, 1, yp)
        rs_core(q, k, 2)
        put(q, k, 2, ())
        rs_hop(q, k, R2B, 2, ym)

    def rs_early(q, k):
        rs_core(q, k, 4)
        put(q, k, 4, ())
        rs_hop(q, k, R4AE, 4, yp, LOW)
        rs_core(q, k, 5)
        put(q, k, 5, ())
        rs_hop(q, k, R4BE, 5, ym, UP)

    def rs_b(q, k):
        rs_core(q, k, 3)
        rs_got(q, k, R1A, UP)
        put(q, k, 3, (R1A,), UP)
        rs_hop(q, k, R3A, 3, yp, UP)
        rs_got(q, k, R1B, LOW)
        put(q, k, 3, (R1B,), LOW)
        rs_hop(q, k, R3B, 3, ym, LOW)

    def rs_b2(q, k):
        rs_core(q, k, 6)
        rs_got(q, k, R2A)
        rs_got(q, k, R2B)
        put(q, k, 6, (R2A, R2B))
        rs_hop(q, k, R5, 6, xp)

    def rs_c(q, k):
        rs_got(q, k, R3A, UP)
        put(q, k, 4, (R3A,), UP, False)
        rs_hop(q, k, R4AL, 4, yp, UP)
        rs_got(q, k, R3B, LOW)
        put(q, k, 5, (R3B,), LOW, False)
        rs_hop(q, k, R4BL, 5, ym, LOW)

    VC = 7

    def rv_start(q):
        xt = xs[q].reshape(2 * TOK, D)
        dv = dvs[q].reshape(2 * TOK, KVW)
        for n in range(4):
            dwv[q, n * 256 : (n + 1) * 256, :] = dot(xt[:, n * 256 : (n + 1) * 256], dv, ((0,), (0,))).astype(bf16)
        for ref, dc in ((pcv, 1), (pov, 0)):
            for i in range(8):
                r = slot(q, *PLACES[i], dc)
                for j in range(4):
                    at_row = pl.multiple_of(r * 64 + 16 * j, 16)
                    ref[q, i, :, j * KVW : (j + 1) * KVW] = dwv[q, pl.ds(at_row, 16), :]
            if dc == 1:
                send(pcv.at[q], rcv.at[q], rv_send.at[q, VC], rv_recv.at[q, VC], cp)

    def rv_a(q):
        arrived(rcv.at[q], rv_recv.at[q, VC])
        for i in range(8):
            pov[q, i] = (pov[q, i].astype(f32) + rcv[q, i].astype(f32)).astype(bf16)
        for i in range(7):
            send(pov.at[q, i], rnv.at[q, i], rv_send.at[q, i], rv_recv.at[q, i], (s, lane(*PLACES[i], 0)))

    def rv_final(q):
        total = pov[q, 7].astype(f32)
        for i in range(7):
            arrived(rnv.at[q, i], rv_recv.at[q, i])
            total = total + rnv[q, i].astype(f32)
        if q == 0:
            finv[...] = total
            store(finv, fv_hbm)
        else:
            msendv[...] = total.astype(bf16)
            send(msendv, mv_hbm, ms_send.at[3], ms_recv.at[3], mir)

    def rs_final(q, k):
        rs_core(q, k, 7)
        rs_got(q, k, R5)
        rs_got(q, k, R4AE, LOW)
        rs_got(q, k, R4BE, UP)
        rs_got(q, k, R4AL, UP)
        rs_got(q, k, R4BL, LOW)
        for rows in (UP, LOW):
            total = add_in(q, k, 7, (R4AL, R4BL, R5), rows)
            here = slice(rows[0], rows[0] + rows[1])
            if q == 0:
                fin[k, here, :] = total
            else:
                msend[k, here, :] = total.astype(bf16)
        if q == 0:
            store(fin.at[k], fo_hbm.at[k])
        else:
            send(msend.at[k], mo_hbm.at[k], ms_send.at[1 + k], ms_recv.at[1 + k], mir)

    own = block(0, OWN)
    send(own, wb.at[1, l], ms_send.at[0], ms_recv.at[0], mir)
    ag_start(0)
    loads[0].wait()
    loads[1].wait()
    softmax(0, 0)
    ag_step1(0)
    softmax(0, 1)
    ag_step1b(0)
    softmax(1, 0)
    ag_step2(0)
    loads[2].wait()
    loads[3].wait()
    loads[4].wait()
    grad_attended(0, (OWN, A, B, X))
    arrived(block(1, OWN), ms_recv.at[0])
    ag_start(1)
    softmax(1, 1)
    ag_step3(0)
    grad_attended(0, (OPP,))
    ag_step1(1)
    grad_attended(0, (AX, BX, OX))
    value_rows(0)
    grad_values(0, 0)
    values(0)
    attended(0, 0)
    ag_step1b(1)
    attended(0, 1)
    ag_step2(1)
    take(0, 0)
    rs_blocks(0, 0)
    rs_a(0, 0)
    take(0, 1)
    rs_blocks(0, 1)
    rs_a(0, 1)
    grad_attended(1, (OWN, A, B, X))
    ag_step3(1)
    score_grads(0, 0, 0)
    rs_b(0, 0)
    rs_early(0, 0)
    grad_attended(1, (OPP, AX, BX, OX))
    value_rows(1)
    grad_values(1, 0)
    rs_b2(0, 0)
    rs_b(0, 1)
    rs_c(0, 0)
    values(1)
    attended(1, 0)
    rs_b2(0, 1)
    rs_early(0, 1)
    attended(1, 1)
    take(1, 0)
    rs_blocks(1, 0)
    rs_a(1, 0)
    take(1, 1)
    rs_blocks(1, 1)
    rs_a(1, 1)
    grad_attended_late(0)
    rs_b(1, 0)
    rs_early(1, 0)
    grad_values(0, 1)
    rv_start(0)
    rs_b2(1, 0)
    grad_attended_late(1)
    rs_b(1, 1)
    grad_values(1, 1)
    rv_start(1)
    rs_early(1, 1)
    rs_b2(1, 1)
    rv_a(0)
    rs_c(1, 0)
    rv_a(1)
    score_grads(0, 0, 1)
    store_scores(0, 0)
    rs_final(1, 0)
    rs_c(1, 1)
    rs_c(0, 1)
    score_grads(1, 0)
    store_scores(1, 0)
    rs_final(1, 1)
    rv_final(1)
    rs_final(0, 0)
    score_grads(1, 1)
    store_scores(1, 1)
    rs_final(0, 1)
    rv_final(0)
    score_grads(0, 1)
    store_scores(0, 1)
    def ending():
        for n in range(2):
            arrived(mo_hbm.at[n], ms_recv.at[1 + n])
        arrived(mv_hbm, ms_recv.at[3])

    def settle():
        for cpy in stores:
            cpy.wait()

    def leave():
        for cpy in sent:
            cpy.wait_send()

    ending()
    settle()
    leave()


def finish(
    wv_in, wo_in, mv_in, mo_in, fo_in, fv_in, ro_in, rv_in, gi_in, dq_in, dk_in,
    gi, dq, dk, wv_new, wo_new, mv_new, mo_new,
    wv, wo, mv, mo, fo, fv, ro, rv, gib, dqb, dkb, wvb, wob, mvb, mob, in_sem, out_sem,
):
    firsts = [(fo_in, fo), (ro_in, ro), (wo_in, wo), (mo_in, mo), (fv_in, fv), (rv_in, rv), (wv_in, wv), (mv_in, mv)]
    pieces = [(dq_in.at[q, t], dqb.at[q, t], dq.at[q, t]) for q in range(2) for t in range(2)]
    pieces += [(gi_in.at[q], gib.at[q], gi.at[q]) for q in range(2)]
    pieces += [(dk_in, dkb, dk)]
    loads = [pltpu.make_async_copy(a, b, in_sem.at[n]) for n, (a, b, *_) in enumerate(firsts + pieces)]
    for cpy in loads:
        cpy.start()
    stores = []

    def store(src, dst):
        cpy = pltpu.make_async_copy(src, dst, out_sem.at[len(stores)])
        cpy.start()
        stores.append(cpy)

    for cpy in loads[:8]:
        cpy.wait()

    def update(total, w, m, w_buf, m_buf, at):
        moment = decay_rate * m[at] + total / LANES
        m_buf[at] = moment
        w_buf[at] = w[at] - learn_rate * moment

    for n in range(2):
        update(fo[n] + ro[n].astype(f32), wo, mo, wob, mob, (slice(None), slice(n * WIDE, (n + 1) * WIDE)))
    store(mob, mo_new)
    store(wob, wo_new)
    total = fv[...] + rv[...].astype(f32)
    for j in range(4):
        update(total[:, j * KVW : (j + 1) * KVW], wv, mv, wvb, mvb, (slice(16 * j, 16 * (j + 1)), slice(None)))
    store(mvb, mv_new)
    store(wvb, wv_new)
    for cpy, (_, b, c) in zip(loads[8:], pieces):
        cpy.wait()
        store(b, c)
    for cpy in stores:
        cpy.wait()


def shards(
    value_weight, out_weight, value_moment, out_moment, inputs_saved, queries_saved, keys_saved,
    grad_now, grad_new, bound_now, bound_new,
):
    sections = lax.axis_size("section")
    hbm = pl.BlockSpec(memory_space=pltpu.MemorySpace.HBM)
    vmem = pl.BlockSpec(memory_space=pltpu.VMEM)
    smem = pl.BlockSpec(memory_space=pltpu.SMEM)
    dma = pltpu.SemaphoreType.DMA
    gi, dq, dk, fo, fv, ro, rv = pl.pallas_call(
        functools.partial(kernel, sections),
        out_shape=(
            jax.ShapeDtypeStruct((2, 2, TOK, D), bf16),
            jax.ShapeDtypeStruct((2, 2, TOK, QW), bf16),
            jax.ShapeDtypeStruct((2, 2, TOK, KVW), bf16),
            jax.ShapeDtypeStruct((2, TOK, WIDE), f32),
            jax.ShapeDtypeStruct((VROWS, D), f32),
            jax.ShapeDtypeStruct((2, TOK, WIDE), bf16),
            jax.ShapeDtypeStruct((VROWS, D), bf16),
        ),
        in_specs=[smem, smem, vmem, vmem, hbm, hbm, hbm, hbm, hbm],
        out_specs=(hbm,) * 7,
        scratch_shapes=[
            pltpu.VMEM((2, LANES, ROWS, D), bf16),
            pltpu.VMEM((2, D, KVW), bf16),
            pltpu.VMEM((2, 2, TOK, D), bf16),
            pltpu.VMEM((2, 2, TOK, QW), bf16),
            pltpu.VMEM((2, 2, TOK, KVW), bf16),
            pltpu.VMEM((2, 2, TOK, D), bf16),
            pltpu.VMEM((2, TOK, D), bf16),
            pltpu.VMEM((2, 2, HEADS, TOK, TOK), f32),
            pltpu.VMEM((2, 2, TOK, KVW), bf16),
            pltpu.VMEM((2, HEADS, 2 * TOK, HS), bf16),
            pltpu.VMEM((2, 2, HEADS, TOK, HS), bf16),
            pltpu.VMEM((2, 2, TOK, KVW), bf16),
            pltpu.VMEM((2, 2, TOK, D), bf16),
            pltpu.VMEM((2, 2, TOK, QW), bf16),
            pltpu.VMEM((2, 2, TOK, KVW), bf16),
            pltpu.VMEM((2, 2, TOK, WIDE), bf16),
            pltpu.VMEM((2, D, KVW), bf16),
            pltpu.VMEM((2, 2, 8, TOK, WIDE), bf16),
            pltpu.VMEM((2, 2, 8, TOK, WIDE), bf16),
            pltpu.VMEM((2, 2, 8, TOK, WIDE), bf16),
            pltpu.VMEM((2, 2, 7, TOK, WIDE), bf16),
            pltpu.VMEM((2, 8, VROWS, D), bf16),
            pltpu.VMEM((2, 8, VROWS, D), bf16),
            pltpu.VMEM((2, 8, VROWS, D), bf16),
            pltpu.VMEM((2, 7, VROWS, D), bf16),
            pltpu.VMEM((2, TOK, WIDE), bf16),
            pltpu.VMEM((VROWS, D), bf16),
            pltpu.VMEM((2, TOK, WIDE), f32),
            pltpu.VMEM((VROWS, D), f32),
            pltpu.VMEM((TOK, TOK), f32),
            dma((5,)),
            dma((15,)),
            dma((2, 18)),
            dma((2, 18)),
            dma((2, 2, 19)),
            dma((2, 2, 19)),
            dma((2, 8)),
            dma((2, 8)),
            dma((4,)),
            dma((4,)),
            dma((2, 2)),
            dma((2, 2)),
        ],
        compiler_params=pltpu.CompilerParams(
            collective_id=0, has_side_effects=True, vmem_limit_bytes=64000 * 1024
        ),
    )(
        bound_now[:, :, 0], bound_new[:, 0], value_weight[0], out_weight[0],
        inputs_saved[:, :, 0], queries_saved[:, :, 0], keys_saved[:, :, 0], grad_now[:, 0], grad_new,
    )
    big = jax.ShapeDtypeStruct((TOK, D), f32)
    small = jax.ShapeDtypeStruct((64, KVW), f32)
    gi, dq, dk, wv, wo, mv, mo = pl.pallas_call(
        finish,
        out_shape=(
            jax.ShapeDtypeStruct((2, 2, TOK, D), bf16),
            jax.ShapeDtypeStruct((2, 2, TOK, QW), bf16),
            jax.ShapeDtypeStruct((2, 2, TOK, KVW), bf16),
            small, big, small, big,
        ),
        in_specs=[hbm] * 11,
        out_specs=(hbm,) * 7,
        scratch_shapes=[
            pltpu.VMEM((64, KVW), f32),
            pltpu.VMEM((TOK, D), f32),
            pltpu.VMEM((64, KVW), f32),
            pltpu.VMEM((TOK, D), f32),
            pltpu.VMEM((2, TOK, WIDE), f32),
            pltpu.VMEM((VROWS, D), f32),
            pltpu.VMEM((2, TOK, WIDE), bf16),
            pltpu.VMEM((VROWS, D), bf16),
            pltpu.VMEM((2, 2, TOK, D), bf16),
            pltpu.VMEM((2, 2, TOK, QW), bf16),
            pltpu.VMEM((2, 2, TOK, KVW), bf16),
            pltpu.VMEM((64, KVW), f32),
            pltpu.VMEM((TOK, D), f32),
            pltpu.VMEM((64, KVW), f32),
            pltpu.VMEM((TOK, D), f32),
            dma((15,)),
            dma((11,)),
        ],
        compiler_params=pltpu.CompilerParams(vmem_limit_bytes=64000 * 1024),
    )(value_weight[0], out_weight[0], value_moment[0], out_moment[0], fo, fv, ro, rv, gi, dq, dk)
    return (gi[:, :, None], dq[:, :, None], dk[:, :, None], wv[None], wo[None], mv[None], mo[None])


def solution(mesh):
    return jax.shard_map(
        shards,
        mesh=mesh,
        in_specs=(
            P("section", "lane", None),
            P("section", "lane", None),
            P("section", "lane", None),
            P("section", "lane", None),
            P(None, None, "section", "lane", None),
            P(None, None, "section", "lane", None),
            P(None, None, "section", "lane", None),
            P(None, "section", "lane", None),
            P(None, "lane", None),
            P(None, None, "lane"),
            P(None, "lane"),
        ),
        out_specs=(
            P(None, None, "section", "lane", None),
            P(None, None, "section", "lane", None),
            P(None, None, "section", "lane", None),
            P("section", "lane", None),
            P("section", "lane", None),
            P("section", "lane", None),
            P("section", "lane", None),
        ),
        check_vma=False,
    )
```

time: 120 us -> 105 us (0.88)
  Pallas kernels: 112 us -> 103 us
  local copies, waits for them, and re-layouts: 3.88 us -> 0 us
  other arithmetic: 3.01 us -> 0 us
    pallas_call x1, Pallas kernels: 112 us -> 98.9 us  [shards(): pl.pallas_call(functools.partial(kernel, sections), out_shape=(jax.ShapeD...]
    pallas_call x0 -> x1, Pallas kernels: none -> 3.9 us  [shards(): pl.pallas_call(finish, out_shape=(jax.ShapeDtypeStruct((2, 2, TOK, D), bf...]
    unnamed x17 -> x0, local copies, waits for them, and re-layouts: 3.02 us -> none
    sub x2 -> x0, other arithmetic: 3.01 us -> none  [the longest x1 2.34 us: shards(): out_weight_new = out_weight - learn_rate * out_moment_new]
where the time goes in v2:
time: 105 us; the launch traced here: 104 us
  Pallas kernels  103 us (98%)
    pallas_call x1, Pallas kernels, shards(): pl.pallas_call(functools.partial(kernel, sections), out_shape=(jax.ShapeD...  98.9 us
    pallas_call x1, Pallas kernels, shards(): pl.pallas_call(finish, out_shape=(jax.ShapeDtypeStruct((2, 2, TOK, D), bf...  3.9 us

profile of v2, /device:TPU:1, one launch (start us, length us, event | category | flops | bytes accessed | tf_op | source)
XLA Modules:
  0.0 103.6 jit_solution(11539664310889955720)
XLA Ops:
  0.6 98.9 %shard_map.162 = (bf16[2,2,128,1024]{3,2,1,0:T(8,128)(2,1)}, bf16[2,2,128,2048]{3,2,1,0:T(8,128)(2,1)}, bf16[2,2,128,256]{3,2,1,0:T(8,128)(2,1)}, f32[2,128,512]...) custom-call(s32[2,16]{1,0:T(2,128)} %bitcast.33, s32[2]{0:T(128)} %bitcast.34, ...), custom_call_target="tpu_custom_call" | custom-call | tf_op jit(solution)/shard_map/pallas_call | solution.py:575
  99.5 3.9 %shard_map.163 = (bf16[2,2,128,1024]{3,2,1,0:T(8,128)(2,1)}, bf16[2,2,128,2048]{3,2,1,0:T(8,128)(2,1)}, bf16[2,2,128,256]{3,2,1,0:T(8,128)(2,1)}, f32[64,256]{1,...) custom-call(f32[64,256]{1,0:T(8,128)} %bitcast.30, f32[128,1024]{1,0:T(8,128)} %bitcast.25, ...), custom_call_target="tpu_custom_call" | custom-call | tf_op jit(solution)/shard_map/pallas_call | solution.py:641

commit v3 on v2

--- a/solution.py
+++ b/solution.py
@@ -19,6 +19,8 @@
 ROWS = 144
 CUT = 80
 VROWS = 16
+SIDE = 16
+UNROLL = 8
 HALF = TOK // 2
 WIDE = D // 2
 
@@ -28,6 +30,7 @@
 bf16 = jnp.bfloat16
 f32 = jnp.float32
 
+VPLACES = ((2, 1), (1, 1), (3, 1), (0, 1), (2, 0), (1, 0), (3, 0), (0, 0))
 PLACES = ((2, 1), (1, 1), (3, 1), (2, 0), (1, 0), (3, 0), (0, 1), (0, 0))
 
 
@@ -37,11 +40,11 @@
 
 def kernel(
     sections,
-    bn, bw, wv_in, wo_in, x_hbm, q_hbm, k_hbm, gnow_hbm, gnew_hbm,
+    bn_in, bw_in, wv_hbm, wo_hbm, x_hbm, q_hbm, k_hbm, gnow_hbm, gnew_hbm,
     gi_hbm, dq_hbm, dk_hbm, fo_hbm, fv_hbm, mo_hbm, mv_hbm,
     wb, wvs, xs, qs, ks, gs, gnews, pr, vs, at, ga, dvs, gis, dqs, dks, rx,
-    dwv, pc, po, rc, rn, pcv, pov, rcv, rnv, msend, msendv, fin, finv, maskb,
-    ld_sem, st_sem, ag_send, ag_recv, rs_send, rs_recv, rv_send, rv_recv, ms_send, ms_recv, nb_send, nb_recv,
+    bn, bw, wv_in, wo_in, dwv, pc, po, rcn, pcv, pov, rvn, msend, msendv, fin, finv, maskb,
+    ld_sem, st_sem, ag_done, ag_recv, rs_done, rs_recv, rv_done, rv_recv, ms_send, ms_recv, nb_done, nb_recv,
 ):
     s = lax.axis_index("section")
     l = lax.axis_index("lane")
@@ -63,11 +66,20 @@
     yp = (s, lane(1, 0, 0))
     ym = (s, lane(3, 0, 0))
     cp = (s, lane(0, 0, 1))
+    y2 = (s, lane(2, 0, 0))
     mir = (sections - 1 - s, lane(0, 1, 0))
     before = ((s + sections - 1) % sections, l)
     after = ((s + 1) % sections, l)
 
+    barrier = pltpu.get_barrier_semaphore()
+    peers = (xp, yp, ym, cp, mir, before, after) + (y2,)
+    for p in peers:
+        pl.semaphore_signal(barrier, inc=1, device_id=p, device_id_type=MESH)
     loads = [
+        pltpu.make_async_copy(wo_hbm, wo_in, ld_sem.at[5]),
+        pltpu.make_async_copy(wv_hbm, wv_in, ld_sem.at[6]),
+        pltpu.make_async_copy(bn_in, bn, ld_sem.at[7]),
+        pltpu.make_async_copy(bw_in, bw, ld_sem.at[8]),
         pltpu.make_async_copy(k_hbm, ks, ld_sem.at[0]),
         pltpu.make_async_copy(q_hbm, qs, ld_sem.at[1]),
         pltpu.make_async_copy(x_hbm, xs, ld_sem.at[2]),
@@ -76,24 +88,18 @@
     ]
     for cpy in loads:
         cpy.start()
-
-    barrier = pltpu.get_barrier_semaphore()
-    peers = (xp, yp, ym, cp, mir, before, after) + tuple((s, lane(dy, dx, 0)) for dy, dx in PLACES[:4])
-    for p in peers:
-        pl.semaphore_signal(barrier, inc=1, device_id=p, device_id_type=MESH)
+    loads[0].wait()
+    loads[1].wait()
     wb[0, l, :TOK, :] = wo_in[...].astype(bf16)
     for j in range(4):
         wb[0, l, TOK:, j * KVW : (j + 1) * KVW] = wv_in[16 * j : 16 * (j + 1), :].astype(bf16)
     pl.semaphore_wait(barrier, len(peers))
-
-    sent = []
 
     def send(src, dst, ssem, rsem, dev):
         cpy = pltpu.make_async_remote_copy(
             src_ref=src, dst_ref=dst, send_sem=ssem, recv_sem=rsem, device_id=dev, device_id_type=MESH
         )
         cpy.start()
-        sent.append(cpy)
 
     def arrived(dst, sem):
         pltpu.make_async_copy(dst, dst, sem).wait()
@@ -106,60 +112,89 @@
     def block(q, kind, core=0):
         return wb.at[q, slot(q, *where_is[kind], core)]
 
-    def ag_send_block(q, n, kind, to, rkind, rows=None):
-        ref = block(q, kind)
-        if rows is not None:
-            ref = ref.at[pl.ds(*rows), :]
-        send(ref, ref, ag_send.at[q, n], ag_recv.at[q, rkind], to)
-
-    def ag_core(q, kind):
-        ref = block(q, kind)
-        send(ref, ref, ag_send.at[q, 8 + kind], ag_recv.at[q, 8 + kind], cp)
+    def piece(q, kind, n, core=0):
+        return block(q, kind, core).at[pl.ds(0, CUT) if n == 0 else pl.ds(CUT, ROWS - CUT), :]
+
+    def most(q, kind):
+        return block(q, kind).at[pl.ds(CUT, TOK - CUT), :]
+
+    def rest(q, kind):
+        return block(q, kind).at[pl.ds(TOK, VROWS), :]
+
+    def ag_send(q, kind, n, to, as_kind):
+        ref = piece(q, kind, n)
+        send(ref, ref, ag_done.at[q], ag_recv.at[q, as_kind * 2 + n], to)
+
+    def ag_send_most(q, kind, to, as_kind):
+        ref = most(q, kind)
+        send(ref, ref, ag_done.at[q], ag_recv.at[q, as_kind * 2 + 1], to)
+
+    def ag_send_rest(q, kind, as_kind):
+        ref = rest(q, kind)
+        send(ref, ref, ag_done.at[q], ag_recv.at[q, 32 + as_kind - AX], xp)
+
+    def ag_core(q, kind, n):
+        ref = piece(q, kind, n)
+        send(ref, ref, ag_done.at[q], ag_recv.at[q, 16 + kind * 2 + n], cp)
+
+    def ag_got(q, kind, n, core=0):
+        arrived(piece(q, kind, n, core), ag_recv.at[q, core * 16 + kind * 2 + n])
 
     def ag_start(q):
-        ag_send_block(q, 0, OWN, yp, 1, (0, CUT))
-        ag_send_block(q, 1, OWN, ym, 2, (CUT, ROWS - CUT))
-        ag_send_block(q, 2, OWN, xp, 0)
-        ag_send_block(q, 16, OWN, yp, 16, (CUT, ROWS - CUT))
-        ag_send_block(q, 17, OWN, ym, 17, (0, CUT))
-        ag_core(q, OWN)
-
-    def part(q, kind, first):
-        return block(q, kind).at[pl.ds(*((0, CUT) if first else (CUT, ROWS - CUT))), :]
+        ag_send(q, OWN, 0, yp, A)
+        ag_send(q, OWN, 1, ym, B)
+        ag_send(q, OWN, 0, xp, X)
+        ag_send(q, OWN, 1, yp, A)
+        ag_send(q, OWN, 0, ym, B)
+        ag_send(q, OWN, 1, xp, X)
+        ag_core(q, OWN, 0)
+        ag_core(q, OWN, 1)
 
     def ag_step1(q):
-        arrived(part(q, A, True), ag_recv.at[q, 1])
-        ag_send_block(q, 3, A, yp, 3, (0, CUT))
-        arrived(part(q, B, False), ag_recv.at[q, 2])
-        ag_send_block(q, 4, B, ym, 4, (CUT, ROWS - CUT))
+        ag_got(q, A, 0)
+        ag_send(q, A, 0, yp, OPP)
+        ag_got(q, B, 1)
+        ag_send(q, B, 1, ym, OPP)
+        ag_core(q, A, 0)
+        ag_core(q, B, 1)
+        ag_got(q, X, 0)
+        ag_send(q, X, 0, yp, AX)
+        ag_send(q, X, 0, ym, BX)
+        ag_core(q, X, 0)
 
     def ag_step1b(q):
-        arrived(block(q, X), ag_recv.at[q, 0])
-        ag_send_block(q, 5, X, yp, 5)
-        ag_send_block(q, 6, X, ym, 6)
-        arrived(part(q, A, False), ag_recv.at[q, 16])
-        ag_core(q, A)
-        arrived(part(q, B, True), ag_recv.at[q, 17])
-        ag_core(q, B)
-        ag_core(q, X)
+        ag_got(q, X, 1)
+        ag_send_most(q, X, yp, AX)
+        ag_send_most(q, X, ym, BX)
+        ag_core(q, X, 1)
+        ag_got(q, A, 1)
+        ag_send_rest(q, A, AX)
+        ag_send_rest(q, B, BX)
+        ag_core(q, A, 1)
+        ag_got(q, B, 0)
+        ag_core(q, B, 0)
 
     def ag_step2(q):
-        arrived(part(q, OPP, True), ag_recv.at[q, 3])
-        arrived(part(q, OPP, False), ag_recv.at[q, 4])
-        ag_send_block(q, 7, OPP, xp, 7)
-        ag_core(q, OPP)
-
-    def ag_step3(q):
-        arrived(block(q, AX), ag_recv.at[q, 5])
-        ag_core(q, AX)
-        arrived(block(q, BX), ag_recv.at[q, 6])
-        ag_core(q, BX)
-        arrived(block(q, OX), ag_recv.at[q, 7])
-        ag_core(q, OX)
+        for n in range(2):
+            ag_got(q, OPP, n)
+            ag_send(q, OPP, n, xp, OX)
+            ag_core(q, OPP, n)
+
+    def ag_step3(q, n):
+        for kind in (AX, BX):
+            if n == 0:
+                ag_got(q, kind, 0)
+            else:
+                arrived(rest(q, kind), ag_recv.at[q, 32 + kind - AX])
+                arrived(most(q, kind), ag_recv.at[q, kind * 2 + 1])
+            ag_core(q, kind, n)
+        ag_got(q, OX, n)
+        ag_core(q, OX, n)
 
     def grad_attended(q, kinds):
         for kind in kinds:
-            arrived(block(q, kind, 1), ag_recv.at[q, 8 + kind])
+            ag_got(q, kind, 0, 1)
+            ag_got(q, kind, 1, 1)
             n = slot(q, *where_is[kind], 0) // 2
             w2 = jnp.concatenate([wb[q, 2 * n, :TOK, :], wb[q, 2 * n + 1, :TOK, :]], axis=0)
             r = dot(gs[q, 0], w2, ((1,), (1,))).astype(bf16)
@@ -195,10 +230,10 @@
         for g in range(2):
             kg = ks[q, t, :, g * HS : (g + 1) * HS]
 
-            @pl.loop(0, GROUP // 2)
+            @pl.loop(0, GROUP // UNROLL)
             def _(n):
-                for u in range(2):
-                    h = g * GROUP + n * 2 + u
+                for u in range(UNROLL):
+                    h = g * GROUP + n * UNROLL + u
                     qh = qs[q, t, :, pl.ds(pl.multiple_of(h * HS, HS), HS)]
                     sc = dot(qh, kg, ((1,), (1,))) * scale + maskb[...]
                     e = jnp.exp(sc - jnp.max(sc, axis=-1, keepdims=True))
@@ -212,14 +247,14 @@
         for g in range(2):
             vg = vs[q, t, :, g * HS : (g + 1) * HS]
 
-            @pl.loop(0, GROUP // 2)
+            @pl.loop(0, GROUP // 4)
             def _(n):
-                for u in range(2):
-                    h = g * GROUP + n * 2 + u
+                for u in range(4):
+                    h = g * GROUP + n * 4 + u
                     at[q, h, t * TOK : (t + 1) * TOK, :] = dot(pr[q, t, h].astype(bf16), vg, ((1,), (0,))).astype(bf16)
 
-    def grad_attended_late(q):
-        @pl.loop(0, HEADS // 2)
+    def grad_attended_late(q, half):
+        @pl.loop(half * HEADS // 4, (half + 1) * HEADS // 4)
         def _(n):
             w2 = jnp.concatenate([wb[q, 2 * n, :TOK, :], wb[q, 2 * n + 1, :TOK, :]], axis=0)
             r = dot(gs[q, 1], w2, ((1,), (1,))).astype(bf16)
@@ -238,7 +273,7 @@
             if t == 0 and n % 2:
                 send(
                     gis.at[q, 0, :, pl.ds(n // 2 * WIDE, WIDE)], rx.at[q, n // 2],
-                    nb_send.at[q, n // 2], nb_recv.at[q, n // 2], before if q == 0 else after,
+                    nb_done.at[q], nb_recv.at[q, n // 2], before if q == 0 else after,
                 )
         store(gis.at[q, t], gi_hbm.at[q, t])
 
@@ -254,8 +289,8 @@
             vg = vs[q, t, :, g * HS : (g + 1) * HS]
 
             def body(n, acc):
-                for u in range(2):
-                    h = g * GROUP + n * 2 + u
+                for u in range(UNROLL):
+                    h = g * GROUP + n * UNROLL + u
                     at_col = pl.ds(pl.multiple_of(h * HS, HS), HS)
                     gp = dot(ga[q, t, h], vg, ((1,), (1,)))
                     p = pr[q, t, h]
@@ -265,7 +300,7 @@
                     acc = acc + dot(ds, qs[q, t, :, at_col], ((0,), (0,)))
                 return acc
 
-            acc = lax.fori_loop(0, GROUP // 2, body, jnp.zeros((TOK, HS), f32))
+            acc = lax.fori_loop(0, GROUP // UNROLL, body, jnp.zeros((TOK, HS), f32))
             dks[q, t, :, g * HS : (g + 1) * HS] = acc.astype(bf16)
 
     def store_scores(q, t):
@@ -281,40 +316,41 @@
 
         for i in places:
             one(pc, i, 1)
-            send(pc.at[q, k, i], rc.at[q, k, i], rs_send.at[q, k, 11 + i], rs_recv.at[q, k, 11 + i], cp)
+            send(pc.at[q, k, i], rcn.at[q, k, i], rs_done.at[q, k], rs_recv.at[q, k, 11 + i], cp)
         for i in places:
             one(po, i, 0)
 
     R1A, R1B, R2A, R2B, R3A, R3B, R4AE, R4AL, R4BE, R4BL, R5 = range(11)
+    X2A, X2B = 19, 20
     UP, LOW, ALL = (0, HALF), (HALF, HALF), (0, TOK)
-    PLACE_OF = {R1A: 0, R1B: 0, R2A: 1, R2B: 2, R3A: 3, R3B: 3, R4AE: 4, R4AL: 4, R4BE: 5, R4BL: 5, R5: 6}
+    PLACE_OF = {R1A: 0, R1B: 0, R2A: 1, R2B: 2, R3A: 3, R3B: 3, R4AE: 4, R4AL: 4, R4BE: 5, R4BL: 5, R5: 6, X2A: 1, X2B: 2}
+    TOP, BOTTOM = (0, SIDE), (TOK - SIDE, SIDE)
+    UNDER, ABOVE = (SIDE, TOK - SIDE), (0, TOK - SIDE)
 
     def rows_of(ref, rows):
         return ref.at[pl.ds(*rows), :]
 
     def rs_core(q, k, i):
-        arrived(rc.at[q, k, i], rs_recv.at[q, k, 11 + i])
+        arrived(rcn.at[q, k, i], rs_recv.at[q, k, 11 + i])
 
     def rs_hop(q, k, n, i, to, rows=ALL):
         send(
-            rows_of(po.at[q, k, i], rows), rows_of(rn.at[q, k, PLACE_OF[n]], rows),
-            rs_send.at[q, k, n], rs_recv.at[q, k, n], to,
+            rows_of(po.at[q, k, i], rows), rows_of(rcn.at[q, k, 8 + PLACE_OF[n]], rows),
+            rs_done.at[q, k], rs_recv.at[q, k, n], to,
         )
 
     def rs_got(q, k, n, rows=ALL):
-        arrived(rows_of(rn.at[q, k, PLACE_OF[n]], rows), rs_recv.at[q, k, n])
-
-    def add_in(q, k, i, more, rows=ALL, core=True):
+        arrived(rows_of(rcn.at[q, k, 8 + PLACE_OF[n]], rows), rs_recv.at[q, k, n])
+
+    def add_in(q, k, i, more, rows=ALL):
         rr = slice(rows[0], rows[0] + rows[1])
-        total = po[q, k, i, rr, :].astype(f32)
-        if core:
-            total = total + rc[q, k, i, rr, :].astype(f32)
+        total = po[q, k, i, rr, :].astype(f32) + rcn[q, k, i, rr, :].astype(f32)
         for n in more:
-            total = total + rn[q, k, PLACE_OF[n], rr, :].astype(f32)
+            total = total + rcn[q, k, 8 + PLACE_OF[n], rr, :].astype(f32)
         return total
 
-    def put(q, k, i, more, rows=ALL, core=True):
-        po[q, k, i, rows[0] : rows[0] + rows[1], :] = add_in(q, k, i, more, rows, core).astype(bf16)
+    def put(q, k, i, more, rows=ALL):
+        po[q, k, i, rows[0] : rows[0] + rows[1], :] = add_in(q, k, i, more, rows).astype(bf16)
 
     def rs_a(q, k):
         rs_core(q, k, 0)
@@ -323,21 +359,22 @@
         rs_hop(q, k, R1B, 0, xp, LOW)
         rs_core(q, k, 1)
         put(q, k, 1, ())
-        rs_hop(q, k, R2A, 1, yp)
+        rs_hop(q, k, R2A, 1, yp, UNDER)
         rs_core(q, k, 2)
         put(q, k, 2, ())
-        rs_hop(q, k, R2B, 2, ym)
+        rs_hop(q, k, R2B, 2, ym, ABOVE)
+        rs_hop(q, k, X2A, 1, xp, TOP)
+        rs_hop(q, k, X2B, 2, xp, BOTTOM)
 
     def rs_early(q, k):
-        rs_core(q, k, 4)
-        put(q, k, 4, ())
+        put(q, k, 4, (), LOW)
         rs_hop(q, k, R4AE, 4, yp, LOW)
-        rs_core(q, k, 5)
-        put(q, k, 5, ())
+        put(q, k, 5, (), UP)
         rs_hop(q, k, R4BE, 5, ym, UP)
 
     def rs_b(q, k):
-        rs_core(q, k, 3)
+        for i in (3, 4, 5):
+            rs_core(q, k, i)
         rs_got(q, k, R1A, UP)
         put(q, k, 3, (R1A,), UP)
         rs_hop(q, k, R3A, 3, yp, UP)
@@ -347,20 +384,25 @@
 
     def rs_b2(q, k):
         rs_core(q, k, 6)
-        rs_got(q, k, R2A)
-        rs_got(q, k, R2B)
-        put(q, k, 6, (R2A, R2B))
+        rs_got(q, k, R2A, UNDER)
+        rs_got(q, k, R2B, ABOVE)
+        put(q, k, 6, (R2B,), TOP)
+        put(q, k, 6, (R2A, R2B), (SIDE, TOK - 2 * SIDE))
+        put(q, k, 6, (R2A,), BOTTOM)
         rs_hop(q, k, R5, 6, xp)
 
     def rs_c(q, k):
+        rs_got(q, k, X2A, TOP)
         rs_got(q, k, R3A, UP)
-        put(q, k, 4, (R3A,), UP, False)
+        put(q, k, 4, (R3A, X2A), TOP)
+        put(q, k, 4, (R3A,), (SIDE, HALF - SIDE))
         rs_hop(q, k, R4AL, 4, yp, UP)
+        rs_got(q, k, X2B, BOTTOM)
         rs_got(q, k, R3B, LOW)
-        put(q, k, 5, (R3B,), LOW, False)
+        put(q, k, 5, (R3B,), (HALF, HALF - SIDE))
+        put(q, k, 5, (R3B, X2B), BOTTOM)
         rs_hop(q, k, R4BL, 5, ym, LOW)
 
-    VC = 7
 
     def rv_start(q):
         xt = xs[q].reshape(2 * TOK, D)
@@ -369,25 +411,31 @@
             dwv[q, n * 256 : (n + 1) * 256, :] = dot(xt[:, n * 256 : (n + 1) * 256], dv, ((0,), (0,))).astype(bf16)
         for ref, dc in ((pcv, 1), (pov, 0)):
             for i in range(8):
-                r = slot(q, *PLACES[i], dc)
+                r = slot(q, *VPLACES[i], dc)
                 for j in range(4):
                     at_row = pl.multiple_of(r * 64 + 16 * j, 16)
                     ref[q, i, :, j * KVW : (j + 1) * KVW] = dwv[q, pl.ds(at_row, 16), :]
             if dc == 1:
-                send(pcv.at[q], rcv.at[q], rv_send.at[q, VC], rv_recv.at[q, VC], cp)
+                send(pcv.at[q], rvn.at[q, pl.ds(0, 8)], rv_done.at[q], rv_recv.at[q, 0], cp)
 
     def rv_a(q):
-        arrived(rcv.at[q], rv_recv.at[q, VC])
+        arrived(rvn.at[q, pl.ds(0, 8)], rv_recv.at[q, 0])
         for i in range(8):
-            pov[q, i] = (pov[q, i].astype(f32) + rcv[q, i].astype(f32)).astype(bf16)
-        for i in range(7):
-            send(pov.at[q, i], rnv.at[q, i], rv_send.at[q, i], rv_recv.at[q, i], (s, lane(*PLACES[i], 0)))
+            pov[q, i] = (pov[q, i].astype(f32) + rvn[q, i].astype(f32)).astype(bf16)
+        send(pov.at[q, pl.ds(0, 4)], rvn.at[q, pl.ds(8, 4)], rv_done.at[q], rv_recv.at[q, 1], xp)
+
+    def rv_b(q):
+        arrived(rvn.at[q, pl.ds(8, 4)], rv_recv.at[q, 1])
+        for i in range(4):
+            pov[q, 4 + i] = (pov[q, 4 + i].astype(f32) + rvn[q, 8 + i].astype(f32)).astype(bf16)
+        for i, to in ((0, y2), (1, yp), (2, ym)):
+            send(pov.at[q, 4 + i], rvn.at[q, 12 + i], rv_done.at[q], rv_recv.at[q, 2 + i], to)
 
     def rv_final(q):
         total = pov[q, 7].astype(f32)
-        for i in range(7):
-            arrived(rnv.at[q, i], rv_recv.at[q, i])
-            total = total + rnv[q, i].astype(f32)
+        for i in range(3):
+            arrived(rvn.at[q, 12 + i], rv_recv.at[q, 2 + i])
+            total = total + rvn[q, 12 + i].astype(f32)
         if q == 0:
             finv[...] = total
             store(finv, fv_hbm)
@@ -415,25 +463,25 @@
             send(msend.at[k], mo_hbm.at[k], ms_send.at[1 + k], ms_recv.at[1 + k], mir)
 
     own = block(0, OWN)
+    ag_start(0)
     send(own, wb.at[1, l], ms_send.at[0], ms_recv.at[0], mir)
-    ag_start(0)
-    loads[0].wait()
-    loads[1].wait()
+    for cpy in loads[2:6]:
+        cpy.wait()
     softmax(0, 0)
+    softmax(0, 1)
     ag_step1(0)
-    softmax(0, 1)
+    softmax(1, 0)
     ag_step1b(0)
-    softmax(1, 0)
+    softmax(1, 1)
     ag_step2(0)
-    loads[2].wait()
-    loads[3].wait()
-    loads[4].wait()
+    for cpy in loads[6:]:
+        cpy.wait()
     grad_attended(0, (OWN, A, B, X))
     arrived(block(1, OWN), ms_recv.at[0])
     ag_start(1)
-    softmax(1, 1)
-    ag_step3(0)
+    ag_step3(0, 0)
     grad_attended(0, (OPP,))
+    ag_step3(0, 1)
     ag_step1(1)
     grad_attended(0, (AX, BX, OX))
     value_rows(0)
@@ -446,62 +494,67 @@
     take(0, 0)
     rs_blocks(0, 0)
     rs_a(0, 0)
+    grad_attended(1, (OWN, A, B, X))
+    ag_step3(1, 0)
     take(0, 1)
     rs_blocks(0, 1)
+    ag_step3(1, 1)
     rs_a(0, 1)
-    grad_attended(1, (OWN, A, B, X))
-    ag_step3(1)
-    score_grads(0, 0, 0)
+    grad_attended(1, (OPP,))
+    grad_attended_late(0, 0)
+    grad_attended(1, (AX, BX, OX))
+    value_rows(1)
+    grad_values(1, 0)
     rs_b(0, 0)
     rs_early(0, 0)
-    grad_attended(1, (OPP, AX, BX, OX))
-    value_rows(1)
-    grad_values(1, 0)
     rs_b2(0, 0)
-    rs_b(0, 1)
-    rs_c(0, 0)
     values(1)
     attended(1, 0)
-    rs_b2(0, 1)
-    rs_early(0, 1)
+    rs_b(0, 1)
     attended(1, 1)
+    rs_c(0, 0)
+    grad_attended_late(0, 1)
     take(1, 0)
     rs_blocks(1, 0)
     rs_a(1, 0)
     take(1, 1)
     rs_blocks(1, 1)
     rs_a(1, 1)
-    grad_attended_late(0)
+    grad_attended_late(1, 0)
     rs_b(1, 0)
+    grad_attended_late(1, 1)
+    grad_values(1, 1)
+    rv_start(1)
+    rs_b2(1, 0)
+    rs_b(1, 1)
     rs_early(1, 0)
+    rs_c(1, 0)
+    rv_a(1)
+    rs_b2(1, 1)
+    rs_early(1, 1)
     grad_values(0, 1)
     rv_start(0)
-    rs_b2(1, 0)
-    grad_attended_late(1)
-    rs_b(1, 1)
-    grad_values(1, 1)
-    rv_start(1)
-    rs_early(1, 1)
-    rs_b2(1, 1)
+    rs_c(1, 1)
+    rs_early(0, 1)
+    rs_b2(0, 1)
+    rv_b(1)
+    rs_c(0, 1)
     rv_a(0)
-    rs_c(1, 0)
-    rv_a(1)
-    score_grads(0, 0, 1)
+    score_grads(0, 0)
     store_scores(0, 0)
     rs_final(1, 0)
-    rs_c(1, 1)
-    rs_c(0, 1)
     score_grads(1, 0)
     store_scores(1, 0)
     rs_final(1, 1)
     rv_final(1)
+    rv_b(0)
     rs_final(0, 0)
     score_grads(1, 1)
     store_scores(1, 1)
     rs_final(0, 1)
-    rv_final(0)
     score_grads(0, 1)
     store_scores(0, 1)
+    rv_final(0)
     def ending():
         for n in range(2):
             arrived(mo_hbm.at[n], ms_recv.at[1 + n])
@@ -512,8 +565,16 @@
             cpy.wait()
 
     def leave():
-        for cpy in sent:
-            cpy.wait_send()
+        for q in range(2):
+            arrived(wb.at[q, pl.ds(0, 15)], ag_done.at[q])
+            for k in range(2):
+                arrived(rcn.at[q, k], rs_done.at[q, k])
+            arrived(rvn.at[q], rv_done.at[q])
+            arrived(rx.at[q], nb_done.at[q])
+        arrived(wb.at[1, 0], ms_send.at[0])
+        for n in range(2):
+            arrived(msend.at[n], ms_send.at[1 + n])
+        arrived(msendv, ms_send.at[3])
 
     ending()
     settle()
@@ -569,8 +630,6 @@
 ):
     sections = lax.axis_size("section")
     hbm = pl.BlockSpec(memory_space=pltpu.MemorySpace.HBM)
-    vmem = pl.BlockSpec(memory_space=pltpu.VMEM)
-    smem = pl.BlockSpec(memory_space=pltpu.SMEM)
     dma = pltpu.SemaphoreType.DMA
     gi, dq, dk, fo, fv, ro, rv = pl.pallas_call(
         functools.partial(kernel, sections),
@@ -583,7 +642,7 @@
             jax.ShapeDtypeStruct((2, TOK, WIDE), bf16),
             jax.ShapeDtypeStruct((VROWS, D), bf16),
         ),
-        in_specs=[smem, smem, vmem, vmem, hbm, hbm, hbm, hbm, hbm],
+        in_specs=[hbm] * 9,
         out_specs=(hbm,) * 7,
         scratch_shapes=[
             pltpu.VMEM((2, LANES, ROWS, D), bf16),
@@ -602,31 +661,33 @@
             pltpu.VMEM((2, 2, TOK, QW), bf16),
             pltpu.VMEM((2, 2, TOK, KVW), bf16),
             pltpu.VMEM((2, 2, TOK, WIDE), bf16),
+            pltpu.SMEM((2, sections), jnp.int32),
+            pltpu.SMEM((2,), jnp.int32),
+            pltpu.VMEM((64, KVW), f32),
+            pltpu.VMEM((TOK, D), f32),
             pltpu.VMEM((2, D, KVW), bf16),
             pltpu.VMEM((2, 2, 8, TOK, WIDE), bf16),
             pltpu.VMEM((2, 2, 8, TOK, WIDE), bf16),
-            pltpu.VMEM((2, 2, 8, TOK, WIDE), bf16),
-            pltpu.VMEM((2, 2, 7, TOK, WIDE), bf16),
+            pltpu.VMEM((2, 2, 15, TOK, WIDE), bf16),
             pltpu.VMEM((2, 8, VROWS, D), bf16),
             pltpu.VMEM((2, 8, VROWS, D), bf16),
-            pltpu.VMEM((2, 8, VROWS, D), bf16),
-            pltpu.VMEM((2, 7, VROWS, D), bf16),
+            pltpu.VMEM((2, 15, VROWS, D), bf16),
             pltpu.VMEM((2, TOK, WIDE), bf16),
             pltpu.VMEM((VROWS, D), bf16),
             pltpu.VMEM((2, TOK, WIDE), f32),
             pltpu.VMEM((VROWS, D), f32),
             pltpu.VMEM((TOK, TOK), f32),
-            dma((5,)),
+            dma((9,)),
             dma((15,)),
-            dma((2, 18)),
-            dma((2, 18)),
-            dma((2, 2, 19)),
-            dma((2, 2, 19)),
-            dma((2, 8)),
-            dma((2, 8)),
+            dma((2,)),
+            dma((2, 34)),
+            dma((2, 2)),
+            dma((2, 2, 21)),
+            dma((2,)),
+            dma((2, 5)),
             dma((4,)),
             dma((4,)),
-            dma((2, 2)),
+            dma((2,)),
             dma((2, 2)),
         ],
         compiler_params=pltpu.CompilerParams(

time: 105 us -> 96.3 us (0.917); the launches traced: 104 us -> 96.2 us
  Pallas kernels: 103 us -> 95.4 us
    pallas_call x1, Pallas kernels: 98.9 us -> 91.5 us  [shards(): pl.pallas_call(functools.partial(kernel, sections), out_shape=(jax.ShapeD...]
where the time goes in v3:
time: 96.3 us; the launch traced here: 96.2 us
  Pallas kernels  95.4 us (99%)
    pallas_call x1, Pallas kernels, shards(): pl.pallas_call(functools.partial(kernel, sections), out_shape=(jax.ShapeD...  91.5 us
    pallas_call x1, Pallas kernels, shards(): pl.pallas_call(finish, out_shape=(jax.ShapeDtypeStruct((2, 2, TOK, D), bf...  3.9 us

profile of v3, /device:TPU:1, one launch (start us, length us, event | category | flops | bytes accessed | tf_op | source)
XLA Modules:
  0.0 96.2 jit_solution(14977037483324429364)
XLA Ops:
  0.6 91.5 %shard_map.162 = (bf16[2,2,128,1024]{3,2,1,0:T(8,128)(2,1)}, bf16[2,2,128,2048]{3,2,1,0:T(8,128)(2,1)}, bf16[2,2,128,256]{3,2,1,0:T(8,128)(2,1)}, f32[2,128,512]...) custom-call(s32[2,16]{1,0:T(2,128)} %bitcast.33, s32[2]{0:T(128)} %bitcast.34, ...), custom_call_target="tpu_custom_call" | custom-call | tf_op jit(solution)/shard_map/pallas_call | solution.py:634
  92.1 3.9 %shard_map.163 = (bf16[2,2,128,1024]{3,2,1,0:T(8,128)(2,1)}, bf16[2,2,128,2048]{3,2,1,0:T(8,128)(2,1)}, bf16[2,2,128,256]{3,2,1,0:T(8,128)(2,1)}, f32[64,256]{1,...) custom-call(f32[64,256]{1,0:T(8,128)} %bitcast.30, f32[128,1024]{1,0:T(8,128)} %bitcast.25, ...), custom_call_target="tpu_custom_call" | custom-call | tf_op jit(solution)/shard_map/pallas_call | solution.py:702

commit v4 on v3

--- a/solution.py
+++ b/solution.py
@@ -511,9 +511,12 @@
     values(1)
     attended(1, 0)
     rs_b(0, 1)
+    grad_attended_late(0, 1)
+    grad_values(0, 1)
+    rv_start(0)
+    rs_c(0, 0)
     attended(1, 1)
-    rs_c(0, 0)
-    grad_attended_late(0, 1)
+    rv_a(0)
     take(1, 0)
     rs_blocks(1, 0)
     rs_a(1, 0)
@@ -532,28 +535,27 @@
     rv_a(1)
     rs_b2(1, 1)
     rs_early(1, 1)
-    grad_values(0, 1)
-    rv_start(0)
     rs_c(1, 1)
+    rs_b2(0, 1)
+    score_grads(0, 0, 0)
+    rs_final(1, 0)
+    rv_b(1)
     rs_early(0, 1)
-    rs_b2(0, 1)
-    rv_b(1)
     rs_c(0, 1)
-    rv_a(0)
-    score_grads(0, 0)
+    rv_b(0)
+    score_grads(0, 0, 1)
     store_scores(0, 0)
-    rs_final(1, 0)
-    score_grads(1, 0)
-    store_scores(1, 0)
+    score_grads(1, 0, 0)
     rs_final(1, 1)
     rv_final(1)
-    rv_b(0)
-    rs_final(0, 0)
+    score_grads(1, 0, 1)
+    store_scores(1, 0)
     score_grads(1, 1)
     store_scores(1, 1)
-    rs_final(0, 1)
+    rs_final(0, 0)
     score_grads(0, 1)
     store_scores(0, 1)
+    rs_final(0, 1)
     rv_final(0)
     def ending():
         for n in range(2):

time: 96.3 us -> 95.3 us (0.990)
  Pallas kernels: 95.4 us -> 94.4 us
    pallas_call x1, Pallas kernels: 91.5 us -> 90.5 us  [shards(): pl.pallas_call(functools.partial(kernel, sections), out_shape=(jax.ShapeD...]
where the time goes in v4:
time: 95.3 us; the launch traced here: 95.2 us
  Pallas kernels  94.4 us (99%)
    pallas_call x1, Pallas kernels, shards(): pl.pallas_call(functools.partial(kernel, sections), out_shape=(jax.ShapeD...  90.5 us
    pallas_call x1, Pallas kernels, shards(): pl.pallas_call(finish, out_shape=(jax.ShapeDtypeStruct((2, 2, TOK, D), bf...  3.9 us

profile of v4, /device:TPU:1, one launch (start us, length us, event | category | flops | bytes accessed | tf_op | source)
XLA Modules:
  0.0 95.2 jit_solution(9548438028824786156)
XLA Ops:
  0.6 90.5 %shard_map.162 = (bf16[2,2,128,1024]{3,2,1,0:T(8,128)(2,1)}, bf16[2,2,128,2048]{3,2,1,0:T(8,128)(2,1)}, bf16[2,2,128,256]{3,2,1,0:T(8,128)(2,1)}, f32[2,128,512]...) custom-call(s32[2,16]{1,0:T(2,128)} %bitcast.33, s32[2]{0:T(128)} %bitcast.34, ...), custom_call_target="tpu_custom_call" | custom-call | tf_op jit(solution)/shard_map/pallas_call | solution.py:636
  91.2 3.9 %shard_map.163 = (bf16[2,2,128,1024]{3,2,1,0:T(8,128)(2,1)}, bf16[2,2,128,2048]{3,2,1,0:T(8,128)(2,1)}, bf16[2,2,128,256]{3,2,1,0:T(8,128)(2,1)}, f32[64,256]{1,...) custom-call(f32[64,256]{1,0:T(8,128)} %bitcast.30, f32[128,1024]{1,0:T(8,128)} %bitcast.25, ...), custom_call_target="tpu_custom_call" | custom-call | tf_op jit(solution)/shard_map/pallas_call | solution.py:704
